TPU v7x, 256 devices: a whole 4x4x8 slice. The times are simulated.
256 devices in a mesh: req: 32 (over x, z), tp: 8 (over y, core).
Axes of the slice: x: 4, y: 4, z: 8, core: 2. Of those that a mesh axis runs over, the one named last changes fastest.
Arguments:
- embeds: bfloat16 [4, 256, 2048], P(None, 'req'), may hold values from -6 to 6
- attn_gain: float32 [2048], replicated, may hold values from 0.1 to 1.9
- qkv_weight: bfloat16 [2048, 3, 2048], P(None, None, 'tp'), may hold values from -0.125 to 0.125
- query_gain: float32 [2048], P('tp'), may hold values from 0.1 to 1.9
- key_gain: float32 [2048], P('tp'), may hold values from 1.5 to 3
- out_weight: bfloat16 [2048, 2048], P('tp'), may hold values from -0.125 to 0.125
- mlp_gain: float32 [2048], replicated, may hold values from 0.1 to 1.9
- router_weight: bfloat16 [2048, 64], replicated, may hold values from -0.25 to 0.25
- gate_up: bfloat16 [64, 2048, 2, 1024], P('req', None, None, 'tp'), may hold values from -0.125 to 0.125
- down_weight: bfloat16 [64, 1024, 2048], P('req', 'tp'), may hold values from -0.1875 to 0.1875
- cache_keys: bfloat16 [131072, 2048], P('req', 'tp')
- cache_values: bfloat16 [131072, 2048], P('req', 'tp'), may hold values from -6 to 6
- tail_keys: bfloat16 [256, 4, 2048], P('req', None, 'tp'), may hold values from -16 to 16
- tail_values: bfloat16 [256, 4, 2048], P('req', None, 'tp'), may hold values from -6 to 6
- parents: int32 [4, 256], P(None, 'req'), may hold values from 0 to 7
- routes: int32 [4, 256, 8], P(None, 'req'), may hold values from 0 to 63, all different within a row; in each aligned block of 8 rows (0 to 7, 8 to 15, ..., all dimensions but the last counted through in order) at most 5 rows name the same one
- group_lengths: int32 [32], replicated, may hold values from 1 to 16384, as said below
- slot_group: int32 [1024], P('req'), may hold values from -1 to 31, as said below
- slot_index: int32 [1024], P('req'), may hold values from 0 to 127, as said below
Outputs:
- hidden_out: bfloat16 [4, 256, 2048], P(None, 'req', 'tp')
- keys_out: bfloat16 [256, 8, 2048], P('req', None, 'tp')
- values_out: bfloat16 [256, 8, 2048], P('req', None, 'tp')
Inputs may be any that keep to these rules, and one draw needn't show every extreme that they name: `parents`: a beam's parent is numbered within its own group. `routes`: each row names 8 different experts; at each step the rows of one index of req (aligned blocks of 8 rows) name one expert at most 5 times, a bound that some block reaches. `group_lengths`: a group of length n holds (n + 127) // 128 pieces. `slot_group`: -1 marks an empty slot; every piece of every group stands in exactly one slot. `slot_index`: 0 in empty slots.
All inputs are finite; a program needn't handle non-finite values.
Results may differ from a plain program's by a relative error of at most 0.015.
The roundings to bfloat16 on the way count: a program that leaves them out, or rounds other values in their place, can miss the bound.
Values may be sent and summed in bfloat16 or wider, within the bound.
A program may use at most 128 MiB of HBM per device.

v0:
```python
import math

import jax
import jax.numpy as jnp
from jax import lax
from jax.sharding import PartitionSpec as P

HD = 128
TOP = 8
BEAMS = 8
PIECE = 128
CAP = 5
STEPS = 4
HIST = 4
TAIL = 8


eps = 1e-05
floor_value = -1e30


def merged_2(part, axis, combine):
    gathered = jax.tree.map(lambda a: lax.all_gather(a, axis), part)

    def take(source):
        return jax.tree.map(lambda a: lax.dynamic_index_in_dim(a, source, 0, False), gathered)

    return lax.fori_loop(
        1, lax.axis_size(axis), lambda source, state: combine(state, take(source)), take(0)
    )


def norm_rows(values, scale_gain):
    mean_square = jnp.mean(values * values, axis=-1, keepdims=True)
    return values * lax.rsqrt(mean_square + eps) * scale_gain


def rotate_heads(values, positions):
    half_size = values.shape[-1] // 2
    freqs = jnp.exp(
        jnp.arange(half_size, dtype=jnp.float32) * (-2.0 * math.log(10000.0) / values.shape[-1])
    )
    angles = positions.astype(jnp.float32)[:, None] * freqs[None, :]
    cosine = jnp.cos(angles)[:, None, :]
    sine = jnp.sin(angles)[:, None, :]
    first_half = values[..., :half_size]
    second_half = values[..., half_size:]
    return jnp.concatenate(
        [first_half * cosine - second_half * sine, second_half * cosine + first_half * sine],
        axis=-1,
    )


def piece_partials(query_groups, lengths, keys_block, values_block, groups_block, index_block):
    safe_group = jnp.maximum(groups_block, 0)
    queries_here = query_groups[safe_group]
    scores = jnp.einsum(
        "sbhd,sphd->sbhp", queries_here, keys_block, preferred_element_type=jnp.float32
    ) * (1.0 / math.sqrt(HD))
    places = index_block[:, None] * PIECE + jnp.arange(PIECE, dtype=jnp.int32)[None, :]
    live = (groups_block[:, None] >= 0) & (places < lengths[safe_group][:, None])
    live_mask = live[:, None, None, :]
    scores = jnp.where(live_mask, scores, floor_value)
    peak = jnp.max(scores, axis=-1)
    weights = jnp.where(live_mask, jnp.exp(scores - peak[..., None]), 0.0)
    weight_sum = jnp.sum(weights, axis=-1)
    blended = jnp.einsum(
        "sbhp,sphd->sbhd",
        weights.astype(jnp.bfloat16),
        values_block,
        preferred_element_type=jnp.float32,
    )
    return (peak, weight_sum, blended)


def join_partials(first, second):
    best = jnp.maximum(first[0], second[0])
    first_factor = jnp.exp(first[0] - best)
    second_factor = jnp.exp(second[0] - best)
    return (
        best,
        first_factor * first[1] + second_factor * second[1],
        first_factor[..., None] * first[2] + second_factor[..., None] * second[2],
    )


def body(
    embeds,
    attn_gain,
    qkv_weight,
    query_gain,
    key_gain,
    out_weight,
    mlp_gain,
    router_weight,
    gate_up,
    down_weight,
    cache_keys,
    cache_values,
    tail_keys,
    tail_values,
    parents,
    routes,
    group_lengths,
    slot_group,
    slot_index,
):
    req_count = lax.axis_size("req")
    req_place = lax.axis_index("req")
    tp_place = lax.axis_index("tp")
    local_rows = embeds.shape[1]
    width = embeds.shape[2]
    col_width = qkv_weight.shape[2]
    heads_here = col_width // HD
    groups_here = local_rows // BEAMS
    groups_all = groups_here * req_count
    experts_here = gate_up.shape[0]
    experts_all = experts_here * req_count
    hidden_here = gate_up.shape[3]
    col_start = tp_place * col_width
    keys_now = jnp.concatenate(
        [tail_keys, jnp.zeros((local_rows, STEPS, col_width), jnp.bfloat16)], axis=1
    )
    values_now = jnp.concatenate(
        [tail_values, jnp.zeros((local_rows, STEPS, col_width), jnp.bfloat16)], axis=1
    )
    local_group = jnp.arange(local_rows, dtype=jnp.int32) // BEAMS
    row_group = req_place * groups_here + local_group
    length_rows = group_lengths[row_group]
    slots_here = slot_group.shape[0]
    cache_k = cache_keys.reshape(slots_here, PIECE, heads_here, HD)
    cache_v = cache_values.reshape(slots_here, PIECE, heads_here, HD)
    group_hot = slot_group[None, :] == jnp.arange(groups_all, dtype=jnp.int32)[:, None]
    hot_float = group_hot.astype(jnp.float32)
    qkv_flat = qkv_weight.reshape(width, 3 * col_width)
    gate_up_flat = gate_up.reshape(experts_here, width, 2 * hidden_here)
    expert_ids = jnp.arange(experts_all, dtype=jnp.int32)
    slot_ids_all = jnp.arange(experts_all * CAP, dtype=jnp.int32)
    results_list = []
    for step_index in range(STEPS):
        inputs = embeds[step_index].astype(jnp.float32)
        normed = norm_rows(inputs, attn_gain).astype(jnp.bfloat16)
        proj = jnp.dot(normed, qkv_flat, preferred_element_type=jnp.float32).reshape(
            local_rows, 3, col_width
        )
        query_raw = proj[:, 0]
        key_raw = proj[:, 1]
        squares = lax.psum(
            (jnp.sum(query_raw * query_raw, axis=1), jnp.sum(key_raw * key_raw, axis=1)), "tp"
        )
        query_normed = query_raw * lax.rsqrt(squares[0][:, None] / width + eps) * query_gain
        key_normed = key_raw * lax.rsqrt(squares[1][:, None] / width + eps) * key_gain
        positions = length_rows + HIST + step_index
        query = rotate_heads(query_normed.reshape(local_rows, heads_here, HD), positions).astype(
            jnp.bfloat16
        )
        key_new = rotate_heads(key_normed.reshape(local_rows, heads_here, HD), positions).astype(
            jnp.bfloat16
        )
        value_new = proj[:, 2].astype(jnp.bfloat16)
        source_rows = local_group * BEAMS + parents[step_index]
        keys_now = (
            keys_now[source_rows]
            .at[:, HIST + step_index]
            .set(key_new.reshape(local_rows, col_width))
        )
        values_now = values_now[source_rows].at[:, HIST + step_index].set(value_new)
        gathered = lax.all_gather(query.reshape(local_rows, col_width), "req", axis=0, tiled=True)
        query_groups = gathered.reshape(groups_all, BEAMS, heads_here, HD)
        peak, weight_sum, blended = piece_partials(
            query_groups, group_lengths, cache_k, cache_v, slot_group, slot_index
        )
        group_peak = jnp.max(
            jnp.where(group_hot[:, :, None, None], peak[None], floor_value), axis=1
        )
        own_peak = group_peak[jnp.maximum(slot_group, 0)]
        factor = jnp.where((slot_group >= 0)[:, None, None], jnp.exp(peak - own_peak), 0.0)
        group_sum = jnp.einsum(
            "gs,sbh->gbh", hot_float, factor * weight_sum, precision=lax.Precision.HIGHEST
        )
        group_blend = jnp.einsum(
            "gs,sbhd->gbhd", hot_float, factor[..., None] * blended, precision=lax.Precision.HIGHEST
        )
        merged = merged_2((group_peak, group_sum, group_blend), "req", join_partials)
        first_group = req_place * groups_here
        cache_peak = lax.dynamic_slice_in_dim(merged[0], first_group, groups_here, 0)
        cache_sum = lax.dynamic_slice_in_dim(merged[1], first_group, groups_here, 0)
        cache_blend = lax.dynamic_slice_in_dim(merged[2], first_group, groups_here, 0)
        tail_k = keys_now.reshape(local_rows, TAIL, heads_here, HD)
        tail_v = values_now.reshape(local_rows, TAIL, heads_here, HD)
        tail_scores = jnp.einsum(
            "rhd,rjhd->rhj", query, tail_k, preferred_element_type=jnp.float32
        ) * (1.0 / math.sqrt(HD))
        tail_live = (jnp.arange(TAIL, dtype=jnp.int32) <= HIST + step_index)[None, None, :]
        tail_scores = jnp.where(tail_live, tail_scores, floor_value)
        tail_peak = jnp.max(tail_scores, axis=-1)
        tail_weights = jnp.where(tail_live, jnp.exp(tail_scores - tail_peak[..., None]), 0.0)
        tail_sum = jnp.sum(tail_weights, axis=-1)
        tail_blend = jnp.einsum(
            "rhj,rjhd->rhd",
            tail_weights.astype(jnp.bfloat16),
            tail_v,
            preferred_element_type=jnp.float32,
        )
        row_peak = cache_peak.reshape(local_rows, heads_here)
        best_peak = jnp.maximum(row_peak, tail_peak)
        cache_factor = jnp.exp(row_peak - best_peak)
        tail_factor = jnp.exp(tail_peak - best_peak)
        numer = (
            cache_factor[..., None] * cache_blend.reshape(local_rows, heads_here, HD)
            + tail_factor[..., None] * tail_blend
        )
        denom = cache_factor * cache_sum.reshape(local_rows, heads_here) + tail_factor * tail_sum
        context = (numer / denom[..., None]).reshape(local_rows, col_width).astype(jnp.bfloat16)
        attn_part = jnp.dot(context, out_weight, preferred_element_type=jnp.float32)
        hidden = inputs + lax.psum(attn_part, "tp")
        mlp_in = norm_rows(hidden, mlp_gain).astype(jnp.bfloat16)
        logits = jnp.dot(mlp_in, router_weight, preferred_element_type=jnp.float32)
        chosen = jnp.take_along_axis(logits, routes[step_index], axis=1)
        probs = jax.nn.softmax(chosen, axis=-1)
        picks = routes[step_index].reshape(local_rows * TOP)
        expert_hot = (picks[:, None] == expert_ids[None, :]).astype(jnp.int32)
        ranks = jnp.sum((jnp.cumsum(expert_hot, axis=0) - expert_hot) * expert_hot, axis=1)
        slot_ids = picks * CAP + ranks
        placing = (slot_ids[None, :] == slot_ids_all[:, None]).astype(jnp.bfloat16)
        feature_count = mlp_in.shape[1]
        sending = (
            jnp.dot(placing, jnp.repeat(mlp_in, TOP, axis=0), preferred_element_type=jnp.float32)
            .astype(jnp.bfloat16)
            .reshape(req_count, experts_here, CAP, feature_count)
        )
        arrived_rows = lax.all_to_all(sending, "req", split_axis=0, concat_axis=0, tiled=True)
        gate_and_up = jnp.einsum(
            "sjcd,jdf->sjcf", arrived_rows, gate_up_flat, preferred_element_type=jnp.float32
        )
        activated = (
            jax.nn.silu(gate_and_up[..., :hidden_here]) * gate_and_up[..., hidden_here:]
        ).astype(jnp.bfloat16)
        partial_out = jnp.einsum(
            "sjcf,jfd->sjcd", activated, down_weight, preferred_element_type=jnp.float32
        )
        reduced = lax.psum_scatter(
            partial_out.astype(jnp.bfloat16), "tp", scatter_dimension=3, tiled=True
        )
        returned = lax.all_to_all(reduced, "req", split_axis=0, concat_axis=0, tiled=True)
        flat_back = returned.reshape(experts_all * CAP, returned.shape[3])
        picked = flat_back[slot_ids].reshape(local_rows, TOP, flat_back.shape[1])
        mixture = jnp.sum(probs[..., None] * picked.astype(jnp.float32), axis=1)
        hidden = lax.dynamic_slice_in_dim(hidden, col_start, col_width, 1)
        combined = hidden + mixture
        results_list.append(combined.astype(jnp.bfloat16))
    return (jnp.stack(results_list), keys_now, values_now)


def solution(mesh):
    in_specs = (
        P(None, "req", None),
        P(),
        P(None, None, "tp"),
        P("tp"),
        P("tp"),
        P("tp", None),
        P(),
        P(),
        P("req", None, None, "tp"),
        P("req", "tp", None),
        P("req", "tp"),
        P("req", "tp"),
        P("req", None, "tp"),
        P("req", None, "tp"),
        P(None, "req"),
        P(None, "req", None),
        P(),
        P("req"),
        P("req"),
    )
    out_specs = (P(None, "req", "tp"), P("req", None, "tp"), P("req", None, "tp"))
    return jax.shard_map(body, mesh=mesh, in_specs=in_specs, out_specs=out_specs, check_vma=False)
```

profile of v0, /device:TPU:32, one launch (start us, length us, event | category | flops | bytes accessed | tf_op | source)
XLA Modules:
  0.0 1417.3 jit_solution(9807523001991099070)
XLA Ops:
  22.1 14.9 %all-reduce.2 = (f32[8]{0:T(128)S(1)}, f32[8]{0:T(128)S(1)}, f32[8]{0:T(128)S(1)}, f32[8]{0:T(128)S(1)}, f32[8]{0:T(128)S(1)}, /*index=5*/f32[8]{0:T(128)S(1)}, f32[8]{0:T(128)S(1)}, f32[8]{0:T(128)S(1)}) all-reduce(f32[8]{0:T(128)S(1)} %get-tuple-element.969, f32[8]{0:T(128)S(1)} %get-tuple-element.971, ...), channel_id=1, replica_groups=mesh['req'=32,'tp'=8] {'tp'}, use_global_device_ids=true, to_apply=%region_9.10 | all-reduce | flops 64 | bytes 512 | tf_op jit(solution)/shard_map/psum | solution.py:148
  40.0 45.4 %all_gather.98 = bf16[256,256]{1,0:T(8,128)(2,1)S(1)} all-gather(bf16[8,256]{1,0:T(8,128)(2,1)S(1)} %fusion.422), channel_id=1, replica_groups=mesh['req'=32,'tp'=8] {'req'}, dimensions={0}, use_global_device_ids=true | all-gather | bytes 135168 | tf_op jit(solution)/shard_map/all_gather | solution.py:168
  89.5 43.8 %all_gather.91 = bf16[256,256]{1,0:T(8,128)(2,1)} all-gather(bf16[8,256]{1,0:T(8,128)(2,1)S(1)} %fusion.424), channel_id=1, replica_groups=mesh['req'=32,'tp'=8] {'req'}, dimensions={0}, use_global_device_ids=true | all-gather | bytes 135168 | tf_op jit(solution)/shard_map/all_gather | solution.py:168
  139.7 45.0 %all_gather.105 = bf16[256,256]{1,0:T(8,128)(2,1)} all-gather(bf16[8,256]{1,0:T(8,128)(2,1)S(1)} %fusion.420), channel_id=1, replica_groups=mesh['req'=32,'tp'=8] {'req'}, dimensions={0}, use_global_device_ids=true | all-gather | bytes 135168 | tf_op jit(solution)/shard_map/all_gather | solution.py:168
  188.3 44.0 %all_gather.84 = bf16[256,256]{1,0:T(8,128)(2,1)} all-gather(bf16[8,256]{1,0:T(8,128)(2,1)S(1)} %fusion.426), channel_id=1, replica_groups=mesh['req'=32,'tp'=8] {'req'}, dimensions={0}, use_global_device_ids=true | all-gather | bytes 135168 | tf_op jit(solution)/shard_map/all_gather | solution.py:168
  262.9 54.1 %all-gather.6 = f32[1024,8,2]{1,2,0:T(2,128)} all-gather(f32[32,8,2]{1,2,0:T(2,128)S(1)} %get-tuple-element.991), channel_id=8, replica_groups=mesh['req'=32,'tp'=8] {'req'}, dimensions={0}, use_global_device_ids=true | all-gather | bytes 67584 | tf_op jit(solution)/shard_map/all_gather | solution.py:23
  318.2 52.7 %all-gather.3 = f32[1024,8,2]{1,2,0:T(2,128)} all-gather(f32[32,8,2]{1,2,0:T(2,128)S(1)} %get-tuple-element.990), channel_id=5, replica_groups=mesh['req'=32,'tp'=8] {'req'}, dimensions={0}, use_global_device_ids=true | all-gather | bytes 67584 | tf_op jit(solution)/shard_map/all_gather | solution.py:23
  372.1 50.2 %all-gather = f32[1024,8,2]{1,2,0:T(2,128)S(1)} all-gather(f32[32,8,2]{1,2,0:T(2,128)S(1)} %get-tuple-element.988), channel_id=2, replica_groups=mesh['req'=32,'tp'=8] {'req'}, dimensions={0}, use_global_device_ids=true | all-gather | bytes 67584 | tf_op jit(solution)/shard_map/all_gather | solution.py:23
  424.9 49.2 %all-gather.9 = f32[1024,8,2]{1,2,0:T(2,128)S(1)} all-gather(f32[32,8,2]{1,2,0:T(2,128)S(1)} %get-tuple-element.989), channel_id=11, replica_groups=mesh['req'=32,'tp'=8] {'req'}, dimensions={0}, use_global_device_ids=true | all-gather | bytes 67584 | tf_op jit(solution)/shard_map/all_gather | solution.py:23
  487.5 49.6 %all-gather.7 = f32[1024,8,2]{1,2,0:T(2,128)S(1)} all-gather(f32[32,8,2]{1,2,0:T(2,128)S(1)} %copy.461), channel_id=9, replica_groups=mesh['req'=32,'tp'=8] {'req'}, dimensions={0}, use_global_device_ids=true | all-gather | bytes 67584 | tf_op jit(solution)/shard_map/all_gather | solution.py:23
  545.2 49.0 %all-gather.4 = f32[1024,8,2]{1,2,0:T(2,128)S(1)} all-gather(f32[32,8,2]{1,2,0:T(2,128)S(1)} %copy.437), channel_id=6, replica_groups=mesh['req'=32,'tp'=8] {'req'}, dimensions={0}, use_global_device_ids=true | all-gather | bytes 67584 | tf_op jit(solution)/shard_map/all_gather | solution.py:23
  603.1 49.9 %all-gather.1 = f32[1024,8,2]{1,2,0:T(2,128)S(1)} all-gather(f32[32,8,2]{1,2,0:T(2,128)S(1)} %copy.413), channel_id=3, replica_groups=mesh['req'=32,'tp'=8] {'req'}, dimensions={0}, use_global_device_ids=true | all-gather | bytes 67584 | tf_op jit(solution)/shard_map/all_gather | solution.py:23
  658.4 48.1 %all-gather.10 = f32[1024,8,2]{1,2,0:T(2,128)S(1)} all-gather(f32[32,8,2]{1,2,0:T(2,128)S(1)} %copy.485), channel_id=12, replica_groups=mesh['req'=32,'tp'=8] {'req'}, dimensions={0}, use_global_device_ids=true | all-gather | bytes 67584 | tf_op jit(solution)/shard_map/all_gather | solution.py:23
  711.6 94.3 %while.86 = (s32[]{:T(128)}, f32[32,8,2]{0,2,1:T(2,128)S(1)}, f32[32,8,2]{0,2,1:T(2,128)S(1)}, f32[32,8,2,128]{3,2,1,0:T(2,128)S(1)}, f32[32,32,8,2]{1,3,2,0:T(2...) while((s32[]{:T(128)}, f32[32,8,2]{0,2,1:T(2,128)S(1)}, ...), condition=%wide.region_47.49_spmd, body=%wide.region_46.48_spmd.sunk | while | flops 199685 | bytes 1339543 | solution.py:28
  807.8 94.3 %while.85 = (s32[]{:T(128)}, f32[32,8,2]{0,2,1:T(2,128)S(1)}, f32[32,8,2]{0,2,1:T(2,128)S(1)}, f32[32,8,2,128]{3,2,1,0:T(2,128)S(1)}, f32[32,32,8,2]{1,3,2,0:T(2...) while((s32[]{:T(128)}, f32[32,8,2]{0,2,1:T(2,128)S(1)}, ...), condition=%wide.region_27.29_spmd, body=%wide.region_26.28_spmd.sunk | while | flops 199685 | bytes 1339543 | solution.py:28
  903.9 94.3 %while.84 = (s32[]{:T(128)}, f32[32,8,2]{0,2,1:T(2,128)S(1)}, f32[32,8,2]{0,2,1:T(2,128)S(1)}, f32[32,8,2,128]{3,2,1,0:T(2,128)S(1)}, f32[32,32,8,2]{1,3,2,0:T(2...) while((s32[]{:T(128)}, f32[32,8,2]{0,2,1:T(2,128)S(1)}, ...), condition=%wide.region_7.8_spmd, body=%wide.region_6.7_spmd.sunk | while | flops 199685 | bytes 1339543 | solution.py:28
  1003.0 94.2 %while.87 = (s32[]{:T(128)}, f32[32,8,2]{0,2,1:T(2,128)S(1)}, f32[32,8,2]{0,2,1:T(2,128)S(1)}, f32[32,8,2,128]{3,2,1,0:T(2,128)S(1)}, f32[32,32,8,2]{1,3,2,0:T(2...) while((s32[]{:T(128)}, f32[32,8,2]{0,2,1:T(2,128)S(1)}, ...), condition=%wide.region_67.69_spmd, body=%wide.region_66.68_spmd.sunk | while | flops 199685 | bytes 1339543 | solution.py:28
  1098.9 61.8 %all-reduce.6.cloned.1.call-done = (f32[8,2048]{1,0:T(8,128)}, f32[8,2048]{1,0:T(8,128)}, f32[8,2048]{1,0:T(8,128)}, f32[8,2048]{1,0:T(8,128)}) async-done(((f32[8,2048]{1,0:T(8,128)}, f32[8,2048]{1,0:T(8,128)}, f32[8,2048]{1,0:T(8,128)}, f32[8,2048]{1,0:T(8,128)}), (f32[8,2048]{1,0:T(8,128)}, f32[8,2048]{1,0:T(8,128)}, f32[8,2048]{1,0:T(8,128)}, f32[8,2048]{1,0:T(8,128)})) %all-reduce.6.cloned.1.call-update) | async-done | bytes 262160 | tf_op jit(solution)/shard_map/psum | solution.py:216
  1169.1 10.1 all-to-all-start
  1194.7 16.6 %all-to-all-done = bf16[32,2,5,2048]{3,1,2,0:T(2,128)(2,1)} async-done(((bf16[32,2,5,2048]{3,1,2,0:T(2,128)(2,1)}), bf16[32,2,5,2048]{3,1,2,0:T(2,128)(2,1)}, u32[]{:S(2)}, u32[]{:S(2)}) %all-to-all-start) | async-done | bytes 1310752 | tf_op jit(solution)/shard_map/all_to_all | solution.py:232
  1232.9 15.6 %all-to-all-done.2 = bf16[32,2,5,2048]{3,1,2,0:T(2,128)(2,1)} async-done(((bf16[32,2,5,2048]{3,1,2,0:T(2,128)(2,1)}), bf16[32,2,5,2048]{3,1,2,0:T(2,128)(2,1)}, u32[]{:S(2)}, u32[]{:S(2)}) %all-to-all-start.2) | async-done | bytes 1310752 | tf_op jit(solution)/shard_map/all_to_all | solution.py:232
  1269.7 15.4 %all-to-all-done.4 = bf16[32,2,5,2048]{3,1,2,0:T(2,128)(2,1)} async-done(((bf16[32,2,5,2048]{3,1,2,0:T(2,128)(2,1)}), bf16[32,2,5,2048]{3,1,2,0:T(2,128)(2,1)}, u32[]{:S(2)}, u32[]{:S(2)}) %all-to-all-start.4) | async-done | bytes 1310752 | tf_op jit(solution)/shard_map/all_to_all | solution.py:232
  1294.7 26.0 %all-to-all-done.6 = bf16[32,2,5,2048]{3,1,2,0:T(2,128)(2,1)} async-done(((bf16[32,2,5,2048]{3,1,2,0:T(2,128)(2,1)}), bf16[32,2,5,2048]{3,1,2,0:T(2,128)(2,1)}, u32[]{:S(2)}, u32[]{:S(2)}) %all-to-all-start.6) | async-done | bytes 1310752 | tf_op jit(solution)/shard_map/all_to_all | solution.py:232
  1351.1 21.6 %reduce-scatter.11.cloned.1.call-done = bf16[32,2,5,256]{3,0,2,1:T(8,128)(2,1)} async-done(((bf16[32,2,5,2048]{3,0,2,1:T(8,128)(2,1)}), bf16[32,2,5,256]{3,0,2,1:T(8,128)(2,1)}) %reduce-scatter.11.cloned.1.call-update) | async-done | bytes 163856 | tf_op jit(solution)/shard_map/reduce_scatter | solution.py:242
  (1182 shorter events, 633.5 us)
Async XLA Ops:
  7.2 1211.8 %copy-start = (bf16[2,128,2048]{2,1,0:T(8,128)(2,1)S(1)}, bf16[2,128,2048]{2,1,0:T(8,128)(2,1)}, u32[]{:S(2)}) copy-start(bf16[2,128,2048]{2,1,0:T(8,128)(2,1)} %param.54) | copy-start | bytes 3145732
  7.2 703.2 %all-gather.21.cloned.1.call-start = ((), (), s32[]{:S(2)}) async-start(), calls=%async_computation.18 | async-start | bytes 8650752 | tf_op jit(solution)/shard_map/all_gather | solution.py:23
  249.6 557.0 %all-gather.19.cloned.1.call-start = ((), (), s32[]{:S(2)}) async-start(), calls=%async_computation.17 | async-start | bytes 8650752 | tf_op jit(solution)/shard_map/all_gather | solution.py:23
  252.6 650.1 %all-gather.17.cloned.1.call-start = ((), (), s32[]{:S(2)}) async-start(), calls=%async_computation.16 | async-start | bytes 8650752 | tf_op jit(solution)/shard_map/all_gather | solution.py:23
  255.4 746.4 %all-gather.23.cloned.1.call-start = ((), (), s32[]{:S(2)}) async-start(), calls=%async_computation.19 | async-start | bytes 8650752 | tf_op jit(solution)/shard_map/all_gather | solution.py:23
  258.3 902.3 %all-reduce.6.cloned.1.call-start = ((), (), s32[]{:S(2)}) async-start(), calls=%async_computation.20 | async-start | bytes 524288 | tf_op jit(solution)/shard_map/psum | solution.py:216
  262.9 211.4 %copy-start.29 = (f32[8,2,128]{2,0,1:T(8,128)S(1)}, f32[8,2,128]{2,0,1:T(8,128)}, u32[]{:S(2)}) copy-start(f32[8,2,128]{2,0,1:T(8,128)} %get-tuple-element.1167) | copy-start | bytes 24580
  262.9 211.6 %copy-start.89 = (s32[8]{0:T(128)S(1)}, s32[8]{0:T(128)}, u32[]{:S(2)}) copy-start(s32[8]{0:T(128)} %get-tuple-element.1171) | copy-start | bytes 100
  262.9 211.6 %copy-start.53 = (f32[8,64]{1,0:T(8,128)S(1)}, f32[8,64]{1,0:T(8,128)}, u32[]{:S(2)}) copy-start(f32[8,64]{1,0:T(8,128)} %copy-done.52) | copy-start | bytes 6148
  262.9 211.6 %copy-start.55 = (f32[8,64]{1,0:T(8,128)S(1)}, f32[8,64]{1,0:T(8,128)}, u32[]{:S(2)}) copy-start(f32[8,64]{1,0:T(8,128)} %copy-done.54) | copy-start | bytes 6148
  262.9 211.8 %copy-start.73 = (bf16[8,4,256]{2,1,0:T(4,128)(2,1)S(1)}, bf16[8,4,256]{2,1,0:T(4,128)(2,1)}, u32[]{:S(2)}) copy-start(bf16[8,4,256]{2,1,0:T(4,128)(2,1)} %param.57) | copy-start | bytes 49156
  709.9 388.9 %copy-start.99 = (s32[64]{0:T(128)}, s32[64]{0:T(128)S(1)}, u32[]{:S(2)}) copy-start(s32[64]{0:T(128)S(1)} %select_reduce_fusion.7) | copy-start | bytes 772
  1169.1 42.2 %all-to-all-start = ((bf16[32,2,5,2048]{3,1,2,0:T(2,128)(2,1)}), bf16[32,2,5,2048]{3,1,2,0:T(2,128)(2,1)}, u32[]{:S(2)}, u32[]{:S(2)}) async-start(bf16[32,2,5,2048]{3,1,2,0:T(2,128)(2,1)} %copy.430), calls=%async_computation | async-start | bytes 2621440 | tf_op jit(solution)/shard_map/all_to_all | solution.py:232
  1211.3 37.3 %all-to-all-start.2 = ((bf16[32,2,5,2048]{3,1,2,0:T(2,128)(2,1)}), bf16[32,2,5,2048]{3,1,2,0:T(2,128)(2,1)}, u32[]{:S(2)}, u32[]{:S(2)}) async-start(bf16[32,2,5,2048]{3,1,2,0:T(2,128)(2,1)} %copy.454), calls=%async_computation.3 | async-start | bytes 2621440 | tf_op jit(solution)/shard_map/all_to_all | solution.py:232
  1216.6 110.7 %reduce-scatter.5.cloned.1.call-start = ((), (), s32[]{:S(2)}) async-start(), calls=%async_computation.12 | async-start | bytes 1474560 | tf_op jit(solution)/shard_map/reduce_scatter | solution.py:242
  1248.6 36.5 %all-to-all-start.4 = ((bf16[32,2,5,2048]{3,1,2,0:T(2,128)(2,1)}), bf16[32,2,5,2048]{3,1,2,0:T(2,128)(2,1)}, u32[]{:S(2)}, u32[]{:S(2)}) async-start(bf16[32,2,5,2048]{3,1,2,0:T(2,128)(2,1)} %copy.478), calls=%async_computation.6 | async-start | bytes 2621440 | tf_op jit(solution)/shard_map/all_to_all | solution.py:232
  1253.9 82.0 %reduce-scatter.7.cloned.1.call-start = ((), (), s32[]{:S(2)}) async-start(), calls=%async_computation.13 | async-start | bytes 1474560 | tf_op jit(solution)/shard_map/reduce_scatter | solution.py:242
  1285.1 35.5 %all-to-all-start.6 = ((bf16[32,2,5,2048]{3,1,2,0:T(2,128)(2,1)}), bf16[32,2,5,2048]{3,1,2,0:T(2,128)(2,1)}, u32[]{:S(2)}, u32[]{:S(2)}) async-start(bf16[32,2,5,2048]{3,1,2,0:T(2,128)(2,1)} %copy.502), calls=%async_computation.9 | async-start | bytes 2621440 | tf_op jit(solution)/shard_map/all_to_all | solution.py:232
  1290.4 58.9 %reduce-scatter.9.cloned.1.call-start = ((), (), s32[]{:S(2)}) async-start(), calls=%async_computation.14 | async-start | bytes 1474560 | tf_op jit(solution)/shard_map/reduce_scatter | solution.py:242
  1294.0 78.7 %reduce-scatter.11.cloned.1.call-start = ((), (), s32[]{:S(2)}) async-start(), calls=%async_computation.15 | async-start | bytes 1474560 | tf_op jit(solution)/shard_map/reduce_scatter | solution.py:242
  1329.1 15.5 %all-to-all-start.1 = ((bf16[32,2,5,256]{3,1,2,0:T(2,128)(2,1)}), bf16[32,2,5,256]{3,1,2,0:T(2,128)(2,1)S(1)}, u32[]{:S(2)}, u32[]{:S(2)}) async-start(bf16[32,2,5,256]{3,1,2,0:T(2,128)(2,1)} %copy.432), calls=%async_computation.2 | async-start | bytes 327680 | tf_op jit(solution)/shard_map/all_to_all | solution.py:245
  1344.6 29.9 %all-to-all-start.3 = ((bf16[32,2,5,256]{3,1,2,0:T(2,128)(2,1)}), bf16[32,2,5,256]{3,1,2,0:T(2,128)(2,1)S(1)}, u32[]{:S(2)}, u32[]{:S(2)}) async-start(bf16[32,2,5,256]{3,1,2,0:T(2,128)(2,1)} %copy.456), calls=%async_computation.5 | async-start | bytes 327680 | tf_op jit(solution)/shard_map/all_to_all | solution.py:245
  1374.5 20.1 %all-to-all-start.5 = ((bf16[32,2,5,256]{3,1,2,0:T(2,128)(2,1)}), bf16[32,2,5,256]{3,1,2,0:T(2,128)(2,1)S(1)}, u32[]{:S(2)}, u32[]{:S(2)}) async-start(bf16[32,2,5,256]{3,1,2,0:T(2,128)(2,1)} %copy.480), calls=%async_computation.8 | async-start | bytes 327680 | tf_op jit(solution)/shard_map/all_to_all | solution.py:245
  1394.6 14.4 %all-to-all-start.7 = ((bf16[32,2,5,256]{3,1,2,0:T(2,128)(2,1)}), bf16[32,2,5,256]{3,1,2,0:T(2,128)(2,1)S(1)}, u32[]{:S(2)}, u32[]{:S(2)}) async-start(bf16[32,2,5,256]{3,1,2,0:T(2,128)(2,1)} %copy.504), calls=%async_computation.11 | async-start | bytes 327680 | tf_op jit(solution)/shard_map/all_to_all | solution.py:245
  (95 other events, 6188.1 us)
Sparse Core Ops, SparseCore 0:
  249.7 98.1 all-gather.20
  350.4 100.3 all-gather.18
  453.4 101.6 all-gather.16
  557.5 98.8 all-gather.22
  1099.0 61.6 all-reduce.5
  1220.7 37.0 reduce-scatter.4
  1260.5 36.5 reduce-scatter.6
  1299.8 36.2 reduce-scatter.8
  1338.8 33.7 reduce-scatter.10
where the time goes:
time: 1440 us; the launch traced here: 1420 us
  blocking collectives  596 us (41%)
  local copies, waits for them, and re-layouts  263 us (18%)
  other arithmetic  252 us (18%)
  waiting for transfers between devices  181 us (13%)
  matrix products  53.7 us (4%)
  starting transfers between devices  51.2 us (4%)
  between operations  15.9 us (1%)
    all_gather x8, blocking collectives, merged_2(): gathered = jax.tree.map(lambda a: lax.all_gather(a, axis), part)  403 us
    all_gather x4, blocking collectives, body(): lax.all_gather(query.reshape(local_rows, col_width), 'req', axis=0, tiled...  178 us
    dynamic_slice x136, local copies, waits for them, and re-layouts, take(): lax.dynamic_index_in_dim(a, source, 0, False)  127 us
    add x124, other arithmetic, join_partials(): first_factor[..., None] * first[2] + second_factor[..., None] * second[2]  122 us
    add x124, other arithmetic, join_partials(): first_factor * first[1] + second_factor * second[1]  93.5 us
    all_to_all x4, waiting for transfers between devices, body(): lax.all_to_all(sending, 'req', split_axis=0, concat_axis=0, tiled=True)  73.7 us
    psum x1, waiting for transfers between devices, body(): hidden = inputs + lax.psum(attn_part, 'tp')  61.8 us
  transfers between devices with their start and end apart: 17, of which 9 were waited for; matrix products, arithmetic and copies ran while one was open for 29% of the time, Pallas kernels for 0%

commit v1 on v0

v1 whole, which is shorter than its diff:
```python
import math

import jax
import jax.numpy as jnp
from jax import lax
from jax.experimental import pallas as pl
from jax.experimental.pallas import tpu as pltpu
from jax.sharding import PartitionSpec as P

HD = 128
BEAMS = 8
PIECE = 128
STEPS = 4
HIST = 4
TAIL = 8
SLOT_BLOCK = 4

eps = 1e-05
floor_value = -1e30
scale = 1.0 / math.sqrt(HD)


def norm_rows(values, scale_gain):
    mean_square = jnp.mean(values * values, axis=-1, keepdims=True)
    return values * lax.rsqrt(mean_square + eps) * scale_gain


def rotate_heads(values, positions):
    half_size = values.shape[-1] // 2
    freqs = jnp.exp(
        jnp.arange(half_size, dtype=jnp.float32) * (-2.0 * math.log(10000.0) / values.shape[-1])
    )
    angles = positions.astype(jnp.float32)[:, None] * freqs[None, :]
    cosine = jnp.cos(angles)[:, None, :]
    sine = jnp.sin(angles)[:, None, :]
    first_half = values[..., :half_size]
    second_half = values[..., half_size:]
    return jnp.concatenate(
        [first_half * cosine - second_half * sine, second_half * cosine + first_half * sine],
        axis=-1,
    )


def dot_t(left, right):
    return lax.dot_general(
        left, right, (((1,), (1,)), ((), ())), preferred_element_type=jnp.float32
    )


def cache_kernel(groups_ref, index_ref, lengths_ref, q_ref, k_ref, v_ref, out_ref, acc):
    rows, cols = q_ref.shape[1], q_ref.shape[2]
    heads = cols // HD
    step = pl.program_id(0)
    lane = lax.broadcasted_iota(jnp.int32, (rows, PIECE), 1)

    @pl.when(step == 0)
    def _():
        @pl.loop(0, q_ref.shape[0])
        def _(g):
            acc[g, :, :cols] = jnp.zeros((rows, cols), jnp.float32)
            acc[g, :, cols:] = jnp.where(lane < heads, floor_value, 0.0)

    found = []
    for j in range(SLOT_BLOCK):
        slot = step * SLOT_BLOCK + j
        group = groups_ref[slot]
        safe = jnp.maximum(group, 0)
        limit = jnp.where(group >= 0, lengths_ref[safe] - index_ref[slot] * PIECE, 0)
        live = lane < limit
        here = pl.ds(j * PIECE, PIECE)
        parts = []
        for h in range(heads):
            cut = pl.ds(h * HD, HD)
            scores = dot_t(q_ref[safe, :, cut], k_ref[here, cut]) * scale
            scores = jnp.where(live, scores, floor_value)
            peak = jnp.max(scores, axis=1, keepdims=True)
            weights = jnp.where(live, jnp.exp(scores - peak), 0.0)
            total = jnp.sum(weights, axis=1, keepdims=True)
            blend = jnp.dot(
                weights.astype(jnp.bfloat16), v_ref[here, cut], preferred_element_type=jnp.float32
            )
            parts.append((peak, total, blend))
        found.append((safe, parts))
    for safe, parts in found:
        stat = acc[safe, :, cols:]
        fresh = stat
        for h, (peak, total, blend) in enumerate(parts):
            cut = pl.ds(h * HD, HD)
            old = stat[:, h : h + 1]
            best = jnp.maximum(old, peak)
            old_factor = jnp.exp(old - best)
            new_factor = jnp.exp(peak - best)
            acc[safe, :, cut] = old_factor * acc[safe, :, cut] + new_factor * blend
            sums = old_factor * stat[:, heads + h : heads + h + 1] + new_factor * total
            fresh = jnp.where(lane == h, best, jnp.where(lane == heads + h, sums, fresh))
        acc[safe, :, cols:] = fresh

    @pl.when(step == pl.num_programs(0) - 1)
    def _():
        words = 2 * heads

        @pl.loop(0, q_ref.shape[0])
        def _(g):
            out_ref[g, :, :cols] = acc[g, :, :cols].astype(jnp.bfloat16)
            stat = acc[g, :, cols:]
            first = stat.astype(jnp.bfloat16).astype(jnp.float32)
            second = (stat - first).astype(jnp.bfloat16).astype(jnp.float32)
            third = stat - first - second
            packed = jnp.where(
                lane < words,
                first,
                jnp.where(
                    lane < 2 * words,
                    pltpu.roll(second, words, 1),
                    jnp.where(lane < 3 * words, pltpu.roll(third, 2 * words, 1), 0.0),
                ),
            )
            out_ref[g, :, cols:] = packed.astype(jnp.bfloat16)


def cache_partials(query_groups, cache_keys, cache_values, slot_group, slot_index, lengths):
    groups, rows, cols = query_groups.shape
    slots = slot_group.shape[0]
    block = SLOT_BLOCK * PIECE
    return pl.pallas_call(
        cache_kernel,
        out_shape=jax.ShapeDtypeStruct((groups, rows, cols + 128), jnp.bfloat16),
        grid_spec=pltpu.PrefetchScalarGridSpec(
            num_scalar_prefetch=3,
            grid=(slots // SLOT_BLOCK,),
            in_specs=[
                pl.BlockSpec((groups, rows, cols), lambda i, *_: (0, 0, 0)),
                pl.BlockSpec((block, cols), lambda i, *_: (i, 0)),
                pl.BlockSpec((block, cols), lambda i, *_: (i, 0)),
            ],
            out_specs=pl.BlockSpec((groups, rows, cols + 128), lambda i, *_: (0, 0, 0)),
            scratch_shapes=[pltpu.VMEM((groups, rows, cols + 128), jnp.float32)],
        ),
    )(slot_group, slot_index, lengths, query_groups, cache_keys, cache_values)


def merge_kernel(part_ref, q_ref, k_ref, v_ref, live_ref, out_ref):
    sources, rows = part_ref.shape[0], part_ref.shape[1]
    cols = q_ref.shape[1]
    heads = cols // HD
    words = 2 * heads
    live = live_ref[...] > 0.5
    stats = []
    for s in range(sources):
        packed = part_ref[s, :, cols:].astype(jnp.float32)
        stats.append(
            packed + pltpu.roll(packed, 128 - words, 1) + pltpu.roll(packed, 128 - 2 * words, 1)
        )
    top = stats[0]
    for s in range(1, sources):
        top = jnp.maximum(top, stats[s])
    for h in range(heads):
        cut = pl.ds(h * HD, HD)
        scores = jnp.where(live, dot_t(q_ref[:, cut], k_ref[:, cut]) * scale, floor_value)
        peak = jnp.max(scores, axis=1, keepdims=True)
        weights = jnp.where(live, jnp.exp(scores - peak), 0.0)
        total = jnp.sum(weights, axis=1, keepdims=True)
        blend = jnp.dot(
            weights.astype(jnp.bfloat16), v_ref[:, cut], preferred_element_type=jnp.float32
        )
        best = jnp.maximum(peak, top[:, h : h + 1])
        factor = jnp.exp(peak - best)
        numer = factor * blend
        denom = factor * total
        for s in range(sources):
            factor = jnp.exp(stats[s][:, h : h + 1] - best)
            numer = numer + factor * part_ref[s, :, cut].astype(jnp.float32)
            denom = denom + factor * stats[s][:, heads + h : heads + h + 1]
        out_ref[:, cut] = (numer / denom).astype(jnp.bfloat16)


def merge_partials(parts, query, keys_all, values_all, live):
    return pl.pallas_call(
        merge_kernel,
        out_shape=jax.ShapeDtypeStruct(query.shape, jnp.bfloat16),
        in_specs=[pl.BlockSpec(memory_space=pltpu.VMEM)] * 5,
        out_specs=pl.BlockSpec(memory_space=pltpu.VMEM),
    )(parts, query, keys_all, values_all, live)


def ancestry(parents):
    beams = jnp.arange(BEAMS, dtype=jnp.int32)

    def follow(table, where):
        return jnp.sum(jnp.where(where[:, None] == beams[None, :], table[None, :], 0), axis=1)

    back = []
    for t in range(STEPS):
        rows = [beams, parents[t]]
        for k in range(2, t + 2):
            rows.append(follow(back[t - 1][k - 1], parents[t]))
        back.append(rows)
    sources = []
    for t in range(STEPS):
        first = back[t][t + 1] * HIST
        columns = [first + j for j in range(HIST)]
        for u in range(STEPS):
            if u <= t:
                columns.append(BEAMS * HIST + u * BEAMS + back[t][t - u])
            else:
                columns.append(jnp.full((BEAMS,), -1, jnp.int32))
        sources.append(jnp.stack(columns, axis=1))
    return jnp.stack(sources)


def body(
    embeds,
    attn_gain,
    qkv_weight,
    query_gain,
    key_gain,
    out_weight,
    mlp_gain,
    router_weight,
    gate_up,
    down_weight,
    cache_keys,
    cache_values,
    tail_keys,
    tail_values,
    parents,
    routes,
    group_lengths,
    slot_group,
    slot_index,
):
    req_place = lax.axis_index("req")
    tp_place = lax.axis_index("tp")
    local_rows = embeds.shape[1]
    width = embeds.shape[2]
    col_width = qkv_weight.shape[2]
    heads_here = col_width // HD
    experts_here = gate_up.shape[0]
    experts_all = router_weight.shape[1]
    hidden_here = gate_up.shape[3]
    rows = STEPS * local_rows

    routes_all = lax.all_gather(
        routes.reshape(rows, routes.shape[2]), "req", axis=0, tiled=True
    )

    inputs = embeds.reshape(rows, width).astype(jnp.float32)
    normed = norm_rows(inputs, attn_gain).astype(jnp.bfloat16)
    proj = jnp.dot(
        normed, qkv_weight.reshape(width, 3 * col_width), preferred_element_type=jnp.float32
    )
    query_raw = proj[:, :col_width]
    key_raw = proj[:, col_width : 2 * col_width]
    value_new = proj[:, 2 * col_width :].astype(jnp.bfloat16)
    squares = lax.psum(
        jnp.stack([jnp.sum(query_raw * query_raw, axis=1), jnp.sum(key_raw * key_raw, axis=1)]),
        "tp",
    )
    query_normed = query_raw * lax.rsqrt(squares[0][:, None] / width + eps) * query_gain
    key_normed = key_raw * lax.rsqrt(squares[1][:, None] / width + eps) * key_gain
    own_length = lax.dynamic_index_in_dim(group_lengths, req_place, 0, False)
    positions = own_length + HIST + jnp.arange(rows, dtype=jnp.int32) // local_rows
    query = (
        rotate_heads(query_normed.reshape(rows, heads_here, HD), positions)
        .astype(jnp.bfloat16)
        .reshape(rows, col_width)
    )
    key_new = (
        rotate_heads(key_normed.reshape(rows, heads_here, HD), positions)
        .astype(jnp.bfloat16)
        .reshape(rows, col_width)
    )
    query_groups = lax.all_gather(query, "req")
    partials = cache_partials(
        query_groups, cache_keys, cache_values, slot_group, slot_index, group_lengths
    )
    arrived = lax.all_to_all(partials, "req", split_axis=0, concat_axis=0, tiled=True)

    keys_all = jnp.concatenate([tail_keys.reshape(local_rows * HIST, col_width), key_new])
    values_all = jnp.concatenate([tail_values.reshape(local_rows * HIST, col_width), value_new])
    spots = jnp.arange(keys_all.shape[0], dtype=jnp.int32)
    sources = ancestry(parents)
    hot = sources[..., None] == spots
    live = jnp.any(hot, axis=2).astype(jnp.float32).reshape(rows, spots.shape[0])
    taking = hot[STEPS - 1].reshape(local_rows * TAIL, spots.shape[0]).astype(jnp.bfloat16)
    out_shape = (local_rows, TAIL, col_width)
    keys_out = (
        jnp.dot(taking, keys_all, preferred_element_type=jnp.float32)
        .astype(jnp.bfloat16)
        .reshape(out_shape)
    )
    values_out = (
        jnp.dot(taking, values_all, preferred_element_type=jnp.float32)
        .astype(jnp.bfloat16)
        .reshape(out_shape)
    )

    context = merge_partials(arrived, query, keys_all, values_all, live)
    attn_part = jnp.dot(context, out_weight, preferred_element_type=jnp.float32)
    hidden = inputs + lax.psum(attn_part, "tp")
    mlp_in = norm_rows(hidden, mlp_gain).astype(jnp.bfloat16)
    mlp_all = lax.all_gather(mlp_in, "req", axis=0, tiled=True)

    logits = jnp.dot(mlp_all, router_weight, preferred_element_type=jnp.float32)
    expert_ids = jnp.arange(experts_all, dtype=jnp.int32)
    named = jnp.any(routes_all[:, :, None] == expert_ids, axis=1)
    chosen = jnp.where(named, logits, floor_value)
    peak = jnp.max(chosen, axis=1, keepdims=True)
    raised = jnp.where(named, jnp.exp(chosen - peak), 0.0)
    probs = raised / jnp.sum(raised, axis=1, keepdims=True)
    activated = []
    for j in range(experts_here):
        share = jnp.sum(
            jnp.where(expert_ids == req_place * experts_here + j, probs, 0.0),
            axis=1,
            keepdims=True,
        )
        gate_and_up = jnp.dot(
            mlp_all,
            gate_up[j].reshape(width, 2 * hidden_here),
            preferred_element_type=jnp.float32,
        )
        product = jax.nn.silu(gate_and_up[:, :hidden_here]) * gate_and_up[:, hidden_here:]
        activated.append((share * product).astype(jnp.bfloat16))
    mixed = jnp.dot(
        jnp.concatenate(activated, axis=1),
        down_weight.reshape(experts_here * hidden_here, width),
        preferred_element_type=jnp.float32,
    ).astype(jnp.bfloat16)
    mixed = lax.psum_scatter(mixed, "req", scatter_dimension=0, tiled=True)
    mixed = lax.psum_scatter(mixed, "tp", scatter_dimension=1, tiled=True)
    own_hidden = lax.dynamic_slice_in_dim(hidden, tp_place * col_width, col_width, 1)
    result = (own_hidden + mixed.astype(jnp.float32)).astype(jnp.bfloat16)
    return (result.reshape(STEPS, local_rows, col_width), keys_out, values_out)


def solution(mesh):
    in_specs = (
        P(None, "req", None),
        P(),
        P(None, None, "tp"),
        P("tp"),
        P("tp"),
        P("tp", None),
        P(),
        P(),
        P("req", None, None, "tp"),
        P("req", "tp", None),
        P("req", "tp"),
        P("req", "tp"),
        P("req", None, "tp"),
        P("req", None, "tp"),
        P(None, "req"),
        P(None, "req", None),
        P(),
        P("req"),
        P("req"),
    )
    out_specs = (P(None, "req", "tp"), P("req", None, "tp"), P("req", None, "tp"))
    return jax.shard_map(body, mesh=mesh, in_specs=in_specs, out_specs=out_specs, check_vma=False)
```

time: 1440 us -> 556 us (0.39); the launches traced: 1420 us -> 555 us
  blocking collectives: 596 us -> 114 us
  local copies, waits for them, and re-layouts: 263 us -> 12.2 us
  other arithmetic: 252 us -> 8.91 us
  waiting for transfers between devices: 181 us -> 353 us
  starting transfers between devices: 51.2 us -> 7.15 us
  matrix products: 53.7 us -> 16.4 us
  Pallas kernels: 0 us -> 27.5 us
    all_gather x12 -> x2, blocking collectives: 581 us -> 99.5 us  [the longest x1 56 us: body(): query_groups = lax.all_gather(query, 'req')]
    reduce_scatter x4 -> x2, waiting for transfers between devices: 21.6 us -> 250 us  [the longest x1 217 us: body(): mixed = lax.psum_scatter(mixed, 'req', scatter_dimension=0, tiled=True)]
    add x256 -> x8, other arithmetic: 216 us -> 0.04 us  [the longest x4 0.02 us: ancestry(): columns = [first + j for j in range(HIST)]]
    dynamic_slice x152 -> x1, local copies, waits for them, and re-layouts: 128 us -> 0.59 us  [body(): own_length = lax.dynamic_index_in_dim(group_lengths, req_place, 0, False)]
    all_to_all x8 -> x1, waiting for transfers between devices: 97.4 us -> 11.3 us  [body(): lax.all_to_all(partials, 'req', split_axis=0, concat_axis=0, tiled=True)]
    all_to_all x8 -> x1, starting transfers between devices: 50.2 us -> 6.98 us  [body(): lax.all_to_all(partials, 'req', split_axis=0, concat_axis=0, tiled=True)]
    reshape x15 -> x4, local copies, waits for them, and re-layouts: 36.3 us -> 0.06 us  [the longest x1 0.02 us: body(): key_normed.reshape(rows, heads_here, HD)]
    dot_general x44 -> x7, matrix products: 50.3 us -> 14 us  [the longest x1 3.76 us: body(): logits = jnp.dot(mlp_all, router_weight, preferred_element_type=jnp.float32)]
  transfers between devices with their start and end apart: 17 -> 5, of which waited for: 9 -> 5; matrix products, arithmetic and copies ran while one was open for 29% -> 2% of each run, Pallas kernels for 0% -> 0%
where the time goes in v1:
time: 556 us; the launch traced here: 555 us
  waiting for transfers between devices  353 us (63%)
  blocking collectives  114 us (21%)
  Pallas kernels  27.5 us (5%)
  matrix products  16.4 us (3%)
  between operations  14.9 us (3%)
  local copies, waits for them, and re-layouts  12.2 us (2%)
  other arithmetic  8.91 us (2%)
  starting transfers between devices  7.15 us (1%)
    reduce_scatter x1, waiting for transfers between devices, body(): mixed = lax.psum_scatter(mixed, 'req', scatter_dimension=0, tiled=True)  217 us
    psum x1, waiting for transfers between devices, body(): hidden = inputs + lax.psum(attn_part, 'tp')  59 us
    all_gather x1, blocking collectives, body(): query_groups = lax.all_gather(query, 'req')  56 us
    all_gather x1, blocking collectives, body(): lax.all_gather(routes.reshape(rows, routes.shape[2]), 'req', axis=0, tile...  43.4 us
    all_gather x1, waiting for transfers between devices, body(): mlp_all = lax.all_gather(mlp_in, 'req', axis=0, tiled=True)  32.9 us
    reduce_scatter x1, waiting for transfers between devices, body(): mixed = lax.psum_scatter(mixed, 'tp', scatter_dimension=1, tiled=True)  32.9 us
    pallas_call x1, Pallas kernels, cache_partials(): pl.pallas_call(cache_kernel, out_shape=jax.ShapeDtypeStruct((groups, rows...  24.7 us
    psum x1, blocking collectives, body(): lax.psum(jnp.stack([jnp.sum(query_raw * query_raw, axis=1), jnp.sum(key_r...  14.9 us
  transfers between devices with their start and end apart: 5, of which 5 were waited for; matrix products, arithmetic and copies ran while one was open for 2% of the time, Pallas kernels for 0%

profile of v1, /device:TPU:32, one launch (start us, length us, event | category | flops | bytes accessed | tf_op | source)
XLA Modules:
  0.0 554.7 jit_solution(6136305743436213007)
XLA Ops:
  7.3 4.8 copy.77
  12.2 2.9 fusion.23
  15.3 14.9 %psum.14 = f32[2,32]{1,0:T(2,128)S(1)} all-reduce(f32[2,32]{1,0:T(2,128)S(1)} %pad_maximum_fusion.2), channel_id=1, replica_groups=mesh['req'=32,'tp'=8] {'tp'}, use_global_device_ids=true, to_apply=%region_3.0 | all-reduce | flops 64 | bytes 512 | tf_op jit(solution)/shard_map/psum | solution.py:255
  32.0 56.0 %all_gather.9.q_ref = bf16[32,32,256]{2,1,0:T(8,128)(2,1)} all-gather(bf16[1,32,256]{2,1,0:T(8,128)(2,1)S(1)} %convert_element_type.86), channel_id=1, replica_groups=mesh['req'=32,'tp'=8] {'req'}, dimensions={0}, use_global_device_ids=true | all-gather | bytes 540672 | tf_op jit(solution)/shard_map/all_gather | solution.py:273
  88.0 24.7 %shard_map.202 = bf16[32,32,384]{2,1,0:T(8,128)(2,1)} custom-call(s32[32]{0:T(128)} %groups_ref.1, s32[32]{0:T(128)} %index_ref.1, s32[32]{0:T(128)} %lengths_ref.1, bf16[32,32,256]{2,1,0:T(8,128)(2,1)} %all_gather.9.q_ref, bf16[4096,256]{1,0:T(8,128)(2,1)} %k_ref.1, bf16[4096,256]{1,0:T(8,128)(2,1)} %v_ref.1), custom_call_target="tpu_custom_call" | custom-call | tf_op jit(solution)/shard_map/pallas_call | solution.py:125
  112.7 7.0 %all-to-all-start = ((bf16[32,32,384]{2,1,0:T(8,128)(2,1)}), bf16[32,32,384]{2,1,0:T(8,128)(2,1)S(1)}, u32[]{:S(2)}, u32[]{:S(2)}) async-start(bf16[32,32,384]{2,1,0:T(8,128)(2,1)} %shard_map.202), calls=%async_computation | async-start | bytes 1572864 | tf_op jit(solution)/shard_map/all_to_all | solution.py:277
  124.4 11.3 %all-to-all-done.part_ref = bf16[32,32,384]{2,1,0:T(8,128)(2,1)S(1)} async-done(((bf16[32,32,384]{2,1,0:T(8,128)(2,1)}), bf16[32,32,384]{2,1,0:T(8,128)(2,1)S(1)}, u32[]{:S(2)}, u32[]{:S(2)}) %all-to-all-start) | async-done | bytes 786464 | tf_op jit(solution)/shard_map/all_to_all | solution.py:277
  135.7 0.9 copy-done.2
  136.6 2.8 shard_map.203
  139.3 2.4 fusion.35
  141.8 59.0 %all-reduce.2.cloned.1.call-done = f32[32,2048]{1,0:T(8,128)} async-done(((f32[32,2048]{1,0:T(8,128)}), f32[32,2048]{1,0:T(8,128)}) %all-reduce.2.cloned.1.call-update) | async-done | bytes 262160 | tf_op jit(solution)/shard_map/psum | solution.py:300
  200.8 1.1 multiply_reduce_fusion
  201.9 1.4 multiply_convert_fusion
  204.2 43.4 %all-gather = s32[32,32,8]{1,2,0:T(8,128)S(1)} all-gather(s32[1,32,8]{1,2,0:T(8,128)S(1)} %copy.92), channel_id=1, replica_groups=mesh['req'=32,'tp'=8] {'req'}, dimensions={0}, use_global_device_ids=true | all-gather | bytes 33792 | tf_op jit(solution)/shard_map/all_gather | solution.py:243
  248.4 1.0 fusion
  249.4 2.5 fusion.33
  251.9 32.9 %all-gather.3.cloned.1.call-done = bf16[1024,2048]{1,0:T(8,128)(2,1)} async-done(((bf16[32,2048]{1,0:T(8,128)(2,1)}), bf16[1024,2048]{1,0:T(8,128)(2,1)}) %all-gather.3.cloned.1.call-update) | async-done | bytes 4194320 | tf_op jit(solution)/shard_map/all_gather | solution.py:302
  284.8 3.8 fusion.34
  288.9 1.3 fusion.3
  290.3 1.3 fusion.6
  291.9 3.2 convolution_convert_fusion
  295.2 217.2 %reduce-scatter.3.cloned.1.call-done = bf16[32,2048]{1,0:T(8,128)(2,1)} async-done(((bf16[1024,2048]{1,0:T(8,128)(2,1)}), bf16[32,2048]{1,0:T(8,128)(2,1)}) %reduce-scatter.3.cloned.1.call-update) | async-done | bytes 131088 | tf_op jit(solution)/shard_map/reduce_scatter | solution.py:330
  513.9 32.9 %reduce-scatter.5.cloned.1.call-done = bf16[32,256]{1,0:T(8,128)(2,1)} async-done(((bf16[32,2048]{1,0:T(8,128)(2,1)}), bf16[32,256]{1,0:T(8,128)(2,1)}) %reduce-scatter.5.cloned.1.call-update) | async-done | bytes 16400 | tf_op jit(solution)/shard_map/reduce_scatter | solution.py:331
  546.9 1.3 fusion.27
  (115 shorter events, 9.8 us)
Async XLA Ops:
  7.2 284.6 %copy-start = (bf16[2,128,2048]{2,1,0:T(8,128)(2,1)S(1)}, bf16[2,128,2048]{2,1,0:T(8,128)(2,1)}, u32[]{:S(2)}) copy-start(bf16[2,128,2048]{2,1,0:T(8,128)(2,1)} %param.28) | copy-start | bytes 3145732
  7.2 4.9 copy-start.4
  7.2 5.0 copy-start.14
  7.2 23.0 %copy-start.16 = (f32[256]{0:T(256)S(1)}, f32[256]{0:T(256)}, u32[]{:S(2)}) copy-start(f32[256]{0:T(256)} %param.23) | copy-start | bytes 3076
  7.2 23.0 %copy-start.17 = (f32[256]{0:T(256)S(1)}, f32[256]{0:T(256)}, u32[]{:S(2)}) copy-start(f32[256]{0:T(256)} %param.22) | copy-start | bytes 3076
  7.2 23.1 %copy-start.18 = (s32[32]{0:T(128)S(1)}, s32[32]{0:T(128)}, u32[]{:S(2)}) copy-start(s32[32]{0:T(128)} %lengths_ref.1) | copy-start | bytes 388
  15.1 104.6 %copy-start.15 = (s32[4,8]{1,0:T(4,128)S(1)}, s32[4,8]{1,0:T(4,128)}, u32[]{:S(2)}) copy-start(s32[4,8]{1,0:T(4,128)} %param.33) | copy-start | bytes 388
  15.1 105.9 %copy-start.12 = (bf16[8,4,256]{2,1,0:T(4,128)(2,1)S(1)}, bf16[8,4,256]{2,1,0:T(4,128)(2,1)}, u32[]{:S(2)}) copy-start(bf16[8,4,256]{2,1,0:T(4,128)(2,1)} %param.31) | copy-start | bytes 49156
  15.2 105.9 %copy-start.13 = (bf16[8,4,256]{2,1,0:T(4,128)(2,1)S(1)}, bf16[8,4,256]{2,1,0:T(4,128)(2,1)}, u32[]{:S(2)}) copy-start(bf16[8,4,256]{2,1,0:T(4,128)(2,1)} %param.32) | copy-start | bytes 49156
  112.7 23.0 %all-to-all-start = ((bf16[32,32,384]{2,1,0:T(8,128)(2,1)}), bf16[32,32,384]{2,1,0:T(8,128)(2,1)S(1)}, u32[]{:S(2)}, u32[]{:S(2)}) async-start(bf16[32,32,384]{2,1,0:T(8,128)(2,1)} %shard_map.202), calls=%async_computation | async-start | bytes 1572864 | tf_op jit(solution)/shard_map/all_to_all | solution.py:277
  119.7 81.1 %all-reduce.2.cloned.1.call-start = ((), (), s32[]{:S(2)}) async-start(), calls=%async_computation.3 | async-start | bytes 524288 | tf_op jit(solution)/shard_map/psum | solution.py:300
  121.1 14.6 %copy-start.9 = (bf16[32,256]{1,0:T(8,128)(2,1)}, bf16[32,256]{1,0:T(8,128)(2,1)S(1)}, u32[]{:S(2)}) copy-start(bf16[32,256]{1,0:T(8,128)(2,1)S(1)} %reshape.425) | copy-start | bytes 49156
  124.4 11.3 %copy-start.7 = (bf16[64,256]{1,0:T(8,128)(2,1)}, bf16[64,256]{1,0:T(8,128)(2,1)S(1)}, u32[]{:S(2)}) copy-start(bf16[64,256]{1,0:T(8,128)(2,1)S(1)} %bitcast_dynamic-update-slice_fusion.k_ref) | copy-start | bytes 98308
  135.7 0.9 copy-start.2
  139.3 110.1 %copy-start.3 = (bf16[2,2048,2,128]{3,2,1,0:T(2,128)(2,1)S(1)}, bf16[2,2048,2,128]{3,2,1,0:T(2,128)(2,1)}, u32[]{:S(2)}) copy-start(bf16[2,2048,2,128]{3,2,1,0:T(2,128)(2,1)} %param.27) | copy-start | bytes 6291460
  141.7 143.1 %all-gather.3.cloned.1.call-start = ((), (), s32[]{:S(2)}) async-start(), calls=%async_computation.4 | async-start | bytes 4325376 | tf_op jit(solution)/shard_map/all_gather | solution.py:302
  203.3 309.1 %reduce-scatter.3.cloned.1.call-start = ((), (), s32[]{:S(2)}) async-start(), calls=%async_computation.5 | async-start | bytes 4325376 | tf_op jit(solution)/shard_map/reduce_scatter | solution.py:330
  251.9 36.9 %copy-start.6 = (bf16[1,2048,2,128]{3,2,1,0:T(2,128)(2,1)S(1)}, bf16[1,2048,2,128]{3,2,1,0:T(2,128)(2,1)}, u32[]{:S(2)}) copy-start(bf16[1,2048,2,128]{3,2,1,0:T(2,128)(2,1)} %get-tuple-element.15) | copy-start | bytes 3145732
  284.8 4.0 copy-start.1
  288.8 1.5 copy-start.5
  291.8 220.6 %copy-start.10 = (bf16[32,256]{1,0:T(8,128)(2,1)S(1)}, bf16[32,256]{1,0:T(8,128)(2,1)}, u32[]{:S(2)}) copy-start(bf16[32,256]{1,0:T(8,128)(2,1)} %copy-done.9) | copy-start | bytes 49156
  291.8 220.6 %copy-start.11 = (pred[4,8,8,64]{3,2,1,0:T(8,128)(4,1)S(1)}, pred[4,8,8,64]{3,2,1,0:T(8,128)(4,1)}, u32[]{:S(2)}) copy-start(pred[4,8,8,64]{3,2,1,0:T(8,128)(4,1)} %get-tuple-element.22) | copy-start | bytes 49156
  291.8 221.4 %copy-start.8 = (bf16[64,256]{1,0:T(8,128)(2,1)S(1)}, bf16[64,256]{1,0:T(8,128)(2,1)}, u32[]{:S(2)}) copy-start(bf16[64,256]{1,0:T(8,128)(2,1)} %copy-done.7) | copy-start | bytes 98308
  295.1 251.8 %reduce-scatter.5.cloned.1.call-start = ((), (), s32[]{:S(2)}) async-start(), calls=%async_computation.6 | async-start | bytes 147456 | tf_op jit(solution)/shard_map/reduce_scatter | solution.py:331
Sparse Core Ops, SparseCore 0:
  141.9 58.8 all-reduce.1
  203.7 81.0 all-gather.2
  295.2 217.1 reduce-scatter.2
  514.7 32.0 reduce-scatter.4

commit v2 on v1

--- a/solution.py
+++ b/solution.py
@@ -183,6 +183,39 @@
     )(parts, query, keys_all, values_all, live)
 
 
+def exchange(values, axis):
+    return lax.all_to_all(values, axis, split_axis=0, concat_axis=0, tiled=True)
+
+
+def send_to_all(values, axis):
+    return exchange(jnp.broadcast_to(values, (lax.axis_size(axis),) + values.shape), axis)
+
+
+def sum_to_owner(values, axis):
+    return jnp.sum(exchange(values, axis).astype(jnp.float32), axis=0)
+
+
+def mix_kernel(act_ref, down_ref, out_ref):
+    out_ref[0] = jnp.dot(
+        act_ref[...], down_ref[...], preferred_element_type=jnp.float32
+    ).astype(jnp.bfloat16)
+
+
+def mix_columns(activated, down_flat, parts):
+    rows, inner = activated.shape
+    cols = down_flat.shape[1] // parts
+    return pl.pallas_call(
+        mix_kernel,
+        out_shape=jax.ShapeDtypeStruct((parts, rows, cols), jnp.bfloat16),
+        grid=(parts,),
+        in_specs=[
+            pl.BlockSpec((rows, inner), lambda i: (0, 0)),
+            pl.BlockSpec((inner, cols), lambda i: (0, i)),
+        ],
+        out_specs=pl.BlockSpec((1, rows, cols), lambda i: (i, 0, 0)),
+    )(activated, down_flat)
+
+
 def ancestry(parents):
     beams = jnp.arange(BEAMS, dtype=jnp.int32)
 
@@ -240,10 +273,6 @@
     hidden_here = gate_up.shape[3]
     rows = STEPS * local_rows
 
-    routes_all = lax.all_gather(
-        routes.reshape(rows, routes.shape[2]), "req", axis=0, tiled=True
-    )
-
     inputs = embeds.reshape(rows, width).astype(jnp.float32)
     normed = norm_rows(inputs, attn_gain).astype(jnp.bfloat16)
     proj = jnp.dot(
@@ -270,11 +299,11 @@
         .astype(jnp.bfloat16)
         .reshape(rows, col_width)
     )
-    query_groups = lax.all_gather(query, "req")
+    query_groups = send_to_all(query, "req")
     partials = cache_partials(
         query_groups, cache_keys, cache_values, slot_group, slot_index, group_lengths
     )
-    arrived = lax.all_to_all(partials, "req", split_axis=0, concat_axis=0, tiled=True)
+    arrived = exchange(partials, "req")
 
     keys_all = jnp.concatenate([tail_keys.reshape(local_rows * HIST, col_width), key_new])
     values_all = jnp.concatenate([tail_values.reshape(local_rows * HIST, col_width), value_new])
@@ -297,24 +326,24 @@
 
     context = merge_partials(arrived, query, keys_all, values_all, live)
     attn_part = jnp.dot(context, out_weight, preferred_element_type=jnp.float32)
-    hidden = inputs + lax.psum(attn_part, "tp")
+    tp_count = lax.axis_size("tp")
+    req_count = lax.axis_size("req")
+    attn_own = sum_to_owner(attn_part.reshape(tp_count, rows // tp_count, width), "tp")
+    hidden = inputs + send_to_all(attn_own, "tp").reshape(rows, width)
     mlp_in = norm_rows(hidden, mlp_gain).astype(jnp.bfloat16)
     mlp_all = lax.all_gather(mlp_in, "req", axis=0, tiled=True)
 
-    logits = jnp.dot(mlp_all, router_weight, preferred_element_type=jnp.float32)
+    logits = jnp.dot(mlp_in, router_weight, preferred_element_type=jnp.float32)
     expert_ids = jnp.arange(experts_all, dtype=jnp.int32)
-    named = jnp.any(routes_all[:, :, None] == expert_ids, axis=1)
+    named = jnp.any(routes.reshape(rows, -1)[:, :, None] == expert_ids, axis=1)
     chosen = jnp.where(named, logits, floor_value)
     peak = jnp.max(chosen, axis=1, keepdims=True)
     raised = jnp.where(named, jnp.exp(chosen - peak), 0.0)
     probs = raised / jnp.sum(raised, axis=1, keepdims=True)
+    shares = exchange(probs.T.reshape(req_count, experts_here, rows), "req")
     activated = []
     for j in range(experts_here):
-        share = jnp.sum(
-            jnp.where(expert_ids == req_place * experts_here + j, probs, 0.0),
-            axis=1,
-            keepdims=True,
-        )
+        share = shares[:, j].reshape(req_count * rows, 1)
         gate_and_up = jnp.dot(
             mlp_all,
             gate_up[j].reshape(width, 2 * hidden_here),
@@ -322,15 +351,15 @@
         )
         product = jax.nn.silu(gate_and_up[:, :hidden_here]) * gate_and_up[:, hidden_here:]
         activated.append((share * product).astype(jnp.bfloat16))
-    mixed = jnp.dot(
+    mixed = mix_columns(
         jnp.concatenate(activated, axis=1),
         down_weight.reshape(experts_here * hidden_here, width),
-        preferred_element_type=jnp.float32,
-    ).astype(jnp.bfloat16)
-    mixed = lax.psum_scatter(mixed, "req", scatter_dimension=0, tiled=True)
-    mixed = lax.psum_scatter(mixed, "tp", scatter_dimension=1, tiled=True)
+        tp_count,
+    )
+    mixed = sum_to_owner(mixed, "tp").astype(jnp.bfloat16)
+    mixed = sum_to_owner(mixed.reshape(req_count, rows, col_width), "req")
     own_hidden = lax.dynamic_slice_in_dim(hidden, tp_place * col_width, col_width, 1)
-    result = (own_hidden + mixed.astype(jnp.float32)).astype(jnp.bfloat16)
+    result = (own_hidden + mixed).astype(jnp.bfloat16)
     return (result.reshape(STEPS, local_rows, col_width), keys_out, values_out)
 
 

time: 556 us -> 324 us (0.58)
  waiting for transfers between devices: 353 us -> 122 us
  blocking collectives: 114 us -> 83.2 us
  starting transfers between devices: 7.15 us -> 30.8 us
  Pallas kernels: 27.5 us -> 34.5 us
    reduce_scatter x2 -> x0, waiting for transfers between devices: 250 us -> none  [the longest x1 217 us: body(): mixed = lax.psum_scatter(mixed, 'req', scatter_dimension=0, tiled=True)]
    all_gather x2 -> x0, blocking collectives: 99.5 us -> none  [the longest x1 56 us: body(): query_groups = lax.all_gather(query, 'req')]
    all_to_all x0 -> x2, blocking collectives: none -> 68.3 us  [exchange(): return lax.all_to_all(values, axis, split_axis=0, concat_axis=0, tiled=True)]
    psum x1 -> x0, waiting for transfers between devices: 59 us -> none  [body(): hidden = inputs + lax.psum(attn_part, 'tp')]
    all_to_all x1 -> x5, waiting for transfers between devices: 11.3 us -> 62 us  [exchange(): return lax.all_to_all(values, axis, split_axis=0, concat_axis=0, tiled=True)]
    all_gather x1, waiting for transfers between devices: 32.9 us -> 60 us  [body(): mlp_all = lax.all_gather(mlp_in, 'req', axis=0, tiled=True)]
    all_to_all x1 -> x5, starting transfers between devices: 6.98 us -> 30.8 us  [exchange(): return lax.all_to_all(values, axis, split_axis=0, concat_axis=0, tiled=True)]
    pallas_call x0 -> x1, Pallas kernels: none -> 7.07 us  [mix_columns(): pl.pallas_call(mix_kernel, out_shape=jax.ShapeDtypeStruct((parts, rows, c...]
  transfers between devices with their start and end apart: 5 -> 6, of which waited for: 5 -> 6; matrix products, arithmetic and copies ran while one was open for 2% -> 3% of each run, Pallas kernels for 0% -> 0%
where the time goes in v2:
time: 324 us; the launch traced here: 322 us
  waiting for transfers between devices  122 us (38%)
  blocking collectives  83.2 us (26%)
  Pallas kernels  34.5 us (11%)
  starting transfers between devices  30.8 us (10%)
  between operations  15.1 us (5%)
  local copies, waits for them, and re-layouts  14.5 us (4%)
  matrix products  11.5 us (4%)
  other arithmetic  10.7 us (3%)
    all_to_all x2, blocking collectives, exchange(): return lax.all_to_all(values, axis, split_axis=0, concat_axis=0, tiled=True)  68.3 us
    all_to_all x5, waiting for transfers between devices, exchange(): return lax.all_to_all(values, axis, split_axis=0, concat_axis=0, tiled=True)  62 us
    all_gather x1, waiting for transfers between devices, body(): mlp_all = lax.all_gather(mlp_in, 'req', axis=0, tiled=True)  60 us
    all_to_all x5, starting transfers between devices, exchange(): return lax.all_to_all(values, axis, split_axis=0, concat_axis=0, tiled=True)  30.8 us
    pallas_call x1, Pallas kernels, cache_partials(): pl.pallas_call(cache_kernel, out_shape=jax.ShapeDtypeStruct((groups, rows...  24.7 us
    psum x1, blocking collectives, body(): lax.psum(jnp.stack([jnp.sum(query_raw * query_raw, axis=1), jnp.sum(key_r...  14.9 us
    pallas_call x1, Pallas kernels, mix_columns(): pl.pallas_call(mix_kernel, out_shape=jax.ShapeDtypeStruct((parts, rows, c...  7.07 us
  transfers between devices with their start and end apart: 6, of which 6 were waited for; matrix products, arithmetic and copies ran while one was open for 3% of the time, Pallas kernels for 0%

profile of v2, /device:TPU:32, one launch (start us, length us, event | category | flops | bytes accessed | tf_op | source)
XLA Modules:
  0.0 322.4 jit_solution(8308793796034909895)
XLA Ops:
  7.2 1.3 dynamic_slice.7
  10.3 4.7 %copy.56 = bf16[2048,3,256]{0,2,1:T(8,128)(2,1)} copy(bf16[2048,3,256]{2,0,1:T(8,128)(2,1)} %param.21) | data formatting | bytes 6291456 | tf_op args[2]
  15.0 2.9 fusion.13
  18.1 14.9 %psum.7 = f32[2,32]{1,0:T(2,128)S(1)} all-reduce(f32[2,32]{1,0:T(2,128)S(1)} %pad_maximum_fusion.4), channel_id=1, replica_groups=mesh['req'=32,'tp'=8] {'tp'}, use_global_device_ids=true, to_apply=%region_3.0 | all-reduce | flops 64 | bytes 512 | tf_op jit(solution)/shard_map/psum | solution.py:284
  34.4 11.3 %all-to-all-start = ((bf16[32,32,256]{2,1,0:T(8,128)(2,1)}), bf16[32,32,256]{2,1,0:T(8,128)(2,1)S(1)}, u32[]{:S(2)}, u32[]{:S(2)}) async-start(bf16[32,32,256]{2,1,0:T(8,128)(2,1)} %broadcast_in_dim.89), calls=%async_computation | async-start | bytes 1048576 | tf_op jit(solution)/shard_map/all_to_all | solution.py:187
  46.4 14.7 %all-to-all-done.q_ref = bf16[32,32,256]{2,1,0:T(8,128)(2,1)S(1)} async-done(((bf16[32,32,256]{2,1,0:T(8,128)(2,1)}), bf16[32,32,256]{2,1,0:T(8,128)(2,1)S(1)}, u32[]{:S(2)}, u32[]{:S(2)}) %all-to-all-start) | async-done | bytes 524320 | tf_op jit(solution)/shard_map/all_to_all | solution.py:187
  61.9 24.7 %shard_map.202 = bf16[32,32,384]{2,1,0:T(8,128)(2,1)} custom-call(s32[32]{0:T(128)} %groups_ref.1, s32[32]{0:T(128)} %index_ref.1, s32[32]{0:T(128)} %lengths_ref.1, bf16[32,32,256]{2,1,0:T(8,128)(2,1)} %copy-done.2, bf16[4096,256]{1,0:T(8,128)(2,1)} %k_ref.1, bf16[4096,256]{1,0:T(8,128)(2,1)} %v_ref.1), custom_call_target="tpu_custom_call" | custom-call | tf_op jit(solution)/shard_map/pallas_call | solution.py:125
  86.6 5.0 %all-to-all-start.1 = ((bf16[32,32,384]{2,1,0:T(8,128)(2,1)}), bf16[32,32,384]{2,1,0:T(8,128)(2,1)S(1)}, u32[]{:S(2)}, u32[]{:S(2)}) async-start(bf16[32,32,384]{2,1,0:T(8,128)(2,1)} %shard_map.202), calls=%async_computation.1 | async-start | bytes 1572864 | tf_op jit(solution)/shard_map/all_to_all | solution.py:187
  94.2 18.0 %all-to-all-done.1.part_ref = bf16[32,32,384]{2,1,0:T(8,128)(2,1)S(1)} async-done(((bf16[32,32,384]{2,1,0:T(8,128)(2,1)}), bf16[32,32,384]{2,1,0:T(8,128)(2,1)S(1)}, u32[]{:S(2)}, u32[]{:S(2)}) %all-to-all-start.1) | async-done | bytes 786464 | tf_op jit(solution)/shard_map/all_to_all | solution.py:187
  113.1 2.8 shard_map.203
  117.0 13.5 %all_to_all.35 = f32[8,4,2048]{2,1,0:T(4,128)S(1)} all-to-all(f32[8,4,2048]{2,1,0:T(4,128)S(1)} %reshape.436), channel_id=1, replica_groups=mesh['req'=32,'tp'=8] {'tp'}, dimensions={0} | all-to-all | bytes 524288 | tf_op jit(solution)/shard_map/all_to_all | solution.py:187
  131.3 3.4 %all-to-all-start.3 = ((f32[8,4,2048]{2,1,0:T(4,128)}), f32[8,4,2048]{2,1,0:T(4,128)S(1)}, u32[]{:S(2)}, u32[]{:S(2)}) async-start(f32[8,4,2048]{2,1,0:T(4,128)} %broadcast_in_dim.98), calls=%async_computation.3 | async-start | bytes 524288 | tf_op jit(solution)/shard_map/all_to_all | solution.py:187
  134.8 7.3 %all-to-all-done.3 = f32[8,4,2048]{2,1,0:T(4,128)S(1)} async-done(((f32[8,4,2048]{2,1,0:T(4,128)}), f32[8,4,2048]{2,1,0:T(4,128)S(1)}, u32[]{:S(2)}, u32[]{:S(2)}) %all-to-all-start.3) | async-done | bytes 262176 | tf_op jit(solution)/shard_map/all_to_all | solution.py:187
  145.6 5.1 %all-to-all-start.4 = ((f32[32,2,32]{2,1,0:T(2,128)}), f32[32,2,32]{2,1,0:T(2,128)S(1)}, u32[]{:S(2)}, u32[]{:S(2)}) async-start(f32[32,2,32]{2,1,0:T(2,128)} %bitcast.30), calls=%async_computation.4 | async-start | bytes 65536 | tf_op jit(solution)/shard_map/all_to_all | solution.py:187
  150.7 2.7 fusion.27
  153.4 6.2 %all-to-all-done.4 = f32[32,2,32]{2,1,0:T(2,128)S(1)} async-done(((f32[32,2,32]{2,1,0:T(2,128)}), f32[32,2,32]{2,1,0:T(2,128)S(1)}, u32[]{:S(2)}, u32[]{:S(2)}) %all-to-all-start.4) | async-done | bytes 8224 | tf_op jit(solution)/shard_map/all_to_all | solution.py:187
  159.8 60.0 %all-gather.2.cloned.1.call-done = bf16[1024,2048]{1,0:T(8,128)(2,1)} async-done(((bf16[32,2048]{1,0:T(8,128)(2,1)}), bf16[1024,2048]{1,0:T(8,128)(2,1)}) %all-gather.2.cloned.1.call-update) | async-done | bytes 4194320 | tf_op jit(solution)/shard_map/all_gather | solution.py:334
  219.9 3.6 %fusion.5 = f32[1024,256]{1,0:T(8,128)S(1)} fusion(bf16[1024,2048]{1,0:T(8,128)(2,1)} %all-gather.2.cloned.1.call-done, bf16[256,8,2,128]{3,2,1,0:T(2,128)(2,1)S(1)} %bitcast.126), kind=kOutput, calls=%fused_computation.7 | convolution fusion | flops 1073741824 | bytes 6291456 | tf_op jit(solution)/shard_map/dot_general | solution.py:347
  223.7 1.3 fusion.2
  226.0 7.1 %shard_map.204 = bf16[8,1024,256]{2,1,0:T(8,128)(2,1)} custom-call(bf16[1024,256]{1,0:T(8,128)(2,1)} %pad_maximum_fusion.act_ref, bf16[256,2048]{1,0:T(8,128)(2,1)} %bitcast.124), custom_call_target="tpu_custom_call" | custom-call | tf_op jit(solution)/shard_map/pallas_call | solution.py:207
  233.1 54.8 %all_to_all.36 = bf16[8,1024,256]{2,1,0:T(8,128)(2,1)} all-to-all(bf16[8,1024,256]{2,1,0:T(8,128)(2,1)} %shard_map.204), channel_id=1, replica_groups=mesh['req'=32,'tp'=8] {'tp'}, dimensions={0} | all-to-all | bytes 8388608 | tf_op jit(solution)/shard_map/all_to_all | solution.py:187
  287.9 3.7 %reduce_sum.141 = bf16[1024,256]{1,0:T(8,128)(2,1)} reduce(bf16[8,1024,256]{2,1,0:T(8,128)(2,1)} %all_to_all.36, bf16[]{:T(256)} %constant.78.clone.1), dimensions={0}, to_apply=%region_16.17 | reduce | flops 1835008 | bytes 4718594 | tf_op jit(solution)/shard_map/reduce_sum | solution.py:195
  291.6 5.9 %all-to-all-start.6 = ((bf16[32,32,256]{2,1,0:T(8,128)(2,1)}), bf16[32,32,256]{2,1,0:T(8,128)(2,1)S(1)}, u32[]{:S(2)}, u32[]{:S(2)}) async-start(bf16[32,32,256]{2,1,0:T(8,128)(2,1)} %bitcast.32), calls=%async_computation.6 | async-start | bytes 1048576 | tf_op jit(solution)/shard_map/all_to_all | solution.py:187
  299.0 15.8 %all-to-all-done.6 = bf16[32,32,256]{2,1,0:T(8,128)(2,1)S(1)} async-done(((bf16[32,32,256]{2,1,0:T(8,128)(2,1)}), bf16[32,32,256]{2,1,0:T(8,128)(2,1)S(1)}, u32[]{:S(2)}, u32[]{:S(2)}) %all-to-all-start.6) | async-done | bytes 524320 | tf_op jit(solution)/shard_map/all_to_all | solution.py:187
  (117 shorter events, 16.5 us)
Async XLA Ops:
  7.2 108.7 %copy-start = (bf16[256,2048]{1,0:T(8,128)(2,1)S(1)}, bf16[256,2048]{1,0:T(8,128)(2,1)}, u32[]{:S(2)}) copy-start(bf16[256,2048]{1,0:T(8,128)(2,1)} %param.24) | copy-start | bytes 3145732
  7.2 7.8 %copy-start.3 = (bf16[4,8,2048]{2,1,0:T(8,128)(2,1)S(1)}, bf16[4,8,2048]{2,1,0:T(8,128)(2,1)}, u32[]{:S(2)}) copy-start(bf16[4,8,2048]{2,1,0:T(8,128)(2,1)} %param.19) | copy-start | bytes 393220
  7.2 7.8 %copy-start.11 = (f32[2048]{0:T(1024)S(1)}, f32[2048]{0:T(1024)}, u32[]{:S(2)}) copy-start(f32[2048]{0:T(1024)} %param.20) | copy-start | bytes 24580
  10.2 22.7 %copy-start.14 = (f32[256]{0:T(256)S(1)}, f32[256]{0:T(256)}, u32[]{:S(2)}) copy-start(f32[256]{0:T(256)} %param.23) | copy-start | bytes 3076
  10.2 22.7 %copy-start.15 = (f32[256]{0:T(256)S(1)}, f32[256]{0:T(256)}, u32[]{:S(2)}) copy-start(f32[256]{0:T(256)} %param.22) | copy-start | bytes 3076
  15.0 30.7 %copy-start.13 = (s32[4,8]{1,0:T(4,128)S(1)}, s32[4,8]{1,0:T(4,128)}, u32[]{:S(2)}) copy-start(s32[4,8]{1,0:T(4,128)} %param.33) | copy-start | bytes 388
  33.5 53.1 %copy-start.7 = (bf16[4,8,2,128]{3,1,2,0:T(8,128)(2,1)}, bf16[4,8,2,128]{3,1,2,0:T(8,128)(2,1)S(1)}, u32[]{:S(2)}) copy-start(bf16[4,8,2,128]{3,1,2,0:T(8,128)(2,1)S(1)} %copy.90) | copy-start | bytes 49156
  34.4 58.2 %copy-start.9 = (bf16[8,4,256]{2,1,0:T(4,128)(2,1)S(1)}, bf16[8,4,256]{2,1,0:T(4,128)(2,1)}, u32[]{:S(2)}) copy-start(bf16[8,4,256]{2,1,0:T(4,128)(2,1)} %param.32) | copy-start | bytes 49156
  34.4 58.2 %copy-start.10 = (bf16[8,4,256]{2,1,0:T(4,128)(2,1)S(1)}, bf16[8,4,256]{2,1,0:T(4,128)(2,1)}, u32[]{:S(2)}) copy-start(bf16[8,4,256]{2,1,0:T(4,128)(2,1)} %param.31) | copy-start | bytes 49156
  34.4 26.7 %all-to-all-start = ((bf16[32,32,256]{2,1,0:T(8,128)(2,1)}), bf16[32,32,256]{2,1,0:T(8,128)(2,1)S(1)}, u32[]{:S(2)}, u32[]{:S(2)}) async-start(bf16[32,32,256]{2,1,0:T(8,128)(2,1)} %broadcast_in_dim.89), calls=%async_computation | async-start | bytes 1048576 | tf_op jit(solution)/shard_map/all_to_all | solution.py:187
  61.1 0.8 copy-start.2
  86.6 55.9 %copy-start.12 = (f32[2048]{0:T(1024)S(1)}, f32[2048]{0:T(1024)}, u32[]{:S(2)}) copy-start(f32[2048]{0:T(1024)} %param.25) | copy-start | bytes 24580
  86.6 56.6 %copy-start.8 = (s32[4,8,8]{2,1,0:T(8,128)S(1)}, s32[4,8,8]{2,1,0:T(8,128)}, u32[]{:S(2)}) copy-start(s32[4,8,8]{2,1,0:T(8,128)} %param.34) | copy-start | bytes 3076
  86.6 56.8 %copy-start.4 = (bf16[2048,64]{0,1:T(8,128)(2,1)S(1)}, bf16[2048,64]{0,1:T(8,128)(2,1)}, u32[]{:S(2)}) copy-start(bf16[2048,64]{0,1:T(8,128)(2,1)} %param.26) | copy-start | bytes 786436
  86.6 25.6 %all-to-all-start.1 = ((bf16[32,32,384]{2,1,0:T(8,128)(2,1)}), bf16[32,32,384]{2,1,0:T(8,128)(2,1)S(1)}, u32[]{:S(2)}, u32[]{:S(2)}) async-start(bf16[32,32,384]{2,1,0:T(8,128)(2,1)} %shard_map.202), calls=%async_computation.1 | async-start | bytes 1572864 | tf_op jit(solution)/shard_map/all_to_all | solution.py:187
  94.2 18.0 %copy-start.5 = (bf16[64,256]{1,0:T(8,128)(2,1)}, bf16[64,256]{1,0:T(8,128)(2,1)S(1)}, u32[]{:S(2)}) copy-start(bf16[64,256]{1,0:T(8,128)(2,1)S(1)} %bitcast_dynamic-update-slice_fusion.k_ref) | copy-start | bytes 98308
  112.2 0.9 copy-start.1
  131.3 10.9 %all-to-all-start.3 = ((f32[8,4,2048]{2,1,0:T(4,128)}), f32[8,4,2048]{2,1,0:T(4,128)S(1)}, u32[]{:S(2)}, u32[]{:S(2)}) async-start(f32[8,4,2048]{2,1,0:T(4,128)} %broadcast_in_dim.98), calls=%async_computation.3 | async-start | bytes 524288 | tf_op jit(solution)/shard_map/all_to_all | solution.py:187
  134.7 85.2 %all-gather.2.cloned.1.call-start = ((), (), s32[]{:S(2)}) async-start(), calls=%async_computation.7 | async-start | bytes 4325376 | tf_op jit(solution)/shard_map/all_gather | solution.py:334
  145.6 14.0 %all-to-all-start.4 = ((f32[32,2,32]{2,1,0:T(2,128)}), f32[32,2,32]{2,1,0:T(2,128)S(1)}, u32[]{:S(2)}, u32[]{:S(2)}) async-start(f32[32,2,32]{2,1,0:T(2,128)} %bitcast.30), calls=%async_computation.4 | async-start | bytes 65536 | tf_op jit(solution)/shard_map/all_to_all | solution.py:187
  219.9 3.8 %copy-start.16 = (bf16[1024,2048]{1,0:T(8,128)(2,1)S(1)}, bf16[1024,2048]{1,0:T(8,128)(2,1)}, u32[]{:S(2)}) copy-start(bf16[1024,2048]{1,0:T(8,128)(2,1)} %all-gather.2.cloned.1.call-done) | copy-start | bytes 12582916
  287.9 10.4 %copy-start.6 = (bf16[64,256]{1,0:T(8,128)(2,1)S(1)}, bf16[64,256]{1,0:T(8,128)(2,1)}, u32[]{:S(2)}) copy-start(bf16[64,256]{1,0:T(8,128)(2,1)} %copy-done.5) | copy-start | bytes 98308
  291.6 23.2 %all-to-all-start.6 = ((bf16[32,32,256]{2,1,0:T(8,128)(2,1)}), bf16[32,32,256]{2,1,0:T(8,128)(2,1)S(1)}, u32[]{:S(2)}, u32[]{:S(2)}) async-start(bf16[32,32,256]{2,1,0:T(8,128)(2,1)} %bitcast.32), calls=%async_computation.6 | async-start | bytes 1048576 | tf_op jit(solution)/shard_map/all_to_all | solution.py:187
Sparse Core Ops, SparseCore 0:
  143.4 76.4 all-gather.1

commit v3 on v2

--- a/solution.py
+++ b/solution.py
@@ -13,7 +13,8 @@
 STEPS = 4
 HIST = 4
 TAIL = 8
-SLOT_BLOCK = 4
+SLOT_BLOCK = 8
+CHUNKS = 2
 
 eps = 1e-05
 floor_value = -1e30
@@ -331,7 +332,11 @@
     attn_own = sum_to_owner(attn_part.reshape(tp_count, rows // tp_count, width), "tp")
     hidden = inputs + send_to_all(attn_own, "tp").reshape(rows, width)
     mlp_in = norm_rows(hidden, mlp_gain).astype(jnp.bfloat16)
-    mlp_all = lax.all_gather(mlp_in, "req", axis=0, tiled=True)
+    chunk = rows // CHUNKS
+    gathered = [
+        lax.all_gather(mlp_in[c * chunk : (c + 1) * chunk], "req", axis=0, tiled=True)
+        for c in range(CHUNKS)
+    ]
 
     logits = jnp.dot(mlp_in, router_weight, preferred_element_type=jnp.float32)
     expert_ids = jnp.arange(experts_all, dtype=jnp.int32)
@@ -341,23 +346,23 @@
     raised = jnp.where(named, jnp.exp(chosen - peak), 0.0)
     probs = raised / jnp.sum(raised, axis=1, keepdims=True)
     shares = exchange(probs.T.reshape(req_count, experts_here, rows), "req")
-    activated = []
-    for j in range(experts_here):
-        share = shares[:, j].reshape(req_count * rows, 1)
-        gate_and_up = jnp.dot(
-            mlp_all,
-            gate_up[j].reshape(width, 2 * hidden_here),
-            preferred_element_type=jnp.float32,
-        )
-        product = jax.nn.silu(gate_and_up[:, :hidden_here]) * gate_and_up[:, hidden_here:]
-        activated.append((share * product).astype(jnp.bfloat16))
-    mixed = mix_columns(
-        jnp.concatenate(activated, axis=1),
-        down_weight.reshape(experts_here * hidden_here, width),
-        tp_count,
-    )
-    mixed = sum_to_owner(mixed, "tp").astype(jnp.bfloat16)
-    mixed = sum_to_owner(mixed.reshape(req_count, rows, col_width), "req")
+    down_flat = down_weight.reshape(experts_here * hidden_here, width)
+    mixed_chunks = []
+    for c in range(CHUNKS):
+        activated = []
+        for j in range(experts_here):
+            share = shares[:, j, c * chunk : (c + 1) * chunk].reshape(req_count * chunk, 1)
+            gate_and_up = jnp.dot(
+                gathered[c],
+                gate_up[j].reshape(width, 2 * hidden_here),
+                preferred_element_type=jnp.float32,
+            )
+            product = jax.nn.silu(gate_and_up[:, :hidden_here]) * gate_and_up[:, hidden_here:]
+            activated.append((share * product).astype(jnp.bfloat16))
+        mixed = mix_columns(jnp.concatenate(activated, axis=1), down_flat, tp_count)
+        mixed = sum_to_owner(mixed, "tp").astype(jnp.bfloat16)
+        mixed_chunks.append(mixed.reshape(req_count, chunk, col_width))
+    mixed = sum_to_owner(jnp.concatenate(mixed_chunks, axis=1), "req")
     own_hidden = lax.dynamic_slice_in_dim(hidden, tp_place * col_width, col_width, 1)
     result = (own_hidden + mixed).astype(jnp.bfloat16)
     return (result.reshape(STEPS, local_rows, col_width), keys_out, values_out)

time: 324 us -> 370 us (1.14)
  waiting for transfers between devices: 122 us -> 207 us
  blocking collectives: 83.2 us -> 28.5 us
  starting transfers between devices: 30.8 us -> 40.2 us
  Pallas kernels: 34.5 us -> 39.6 us
    all_gather x1 -> x2, waiting for transfers between devices: 60 us -> 118 us  [body(): lax.all_gather(mlp_in[c * chunk:(c + 1) * chunk], 'req', axis=0, tiled=True)]
    all_to_all x2 -> x1, blocking collectives: 68.3 us -> 13.7 us  [exchange(): return lax.all_to_all(values, axis, split_axis=0, concat_axis=0, tiled=True)]
    all_to_all x5 -> x7, waiting for transfers between devices: 62 us -> 88.9 us  [exchange(): return lax.all_to_all(values, axis, split_axis=0, concat_axis=0, tiled=True)]
    all_to_all x5 -> x7, starting transfers between devices: 30.8 us -> 40.2 us  [exchange(): return lax.all_to_all(values, axis, split_axis=0, concat_axis=0, tiled=True)]
    pallas_call x1 -> x2, Pallas kernels: 7.07 us -> 12.7 us  [mix_columns(): pl.pallas_call(mix_kernel, out_shape=jax.ShapeDtypeStruct((parts, rows, c...]
  transfers between devices with their start and end apart: 6 -> 9, of which waited for: 6 -> 8; matrix products, arithmetic and copies ran while one was open for 3% -> 5% of each run, Pallas kernels for 0% -> 3%
where the time goes in v3:
time: 370 us; the launch traced here: 369 us
  waiting for transfers between devices  207 us (56%)
  starting transfers between devices  40.2 us (11%)
  Pallas kernels  39.6 us (11%)
  blocking collectives  28.5 us (8%)
  between operations  15.2 us (4%)
  local copies, waits for them, and re-layouts  14.9 us (4%)
  matrix products  12.3 us (3%)
  other arithmetic  10.8 us (3%)
    all_gather x2, waiting for transfers between devices, body(): lax.all_gather(mlp_in[c * chunk:(c + 1) * chunk], 'req', axis=0, tiled=True)  118 us
    all_to_all x7, waiting for transfers between devices, exchange(): return lax.all_to_all(values, axis, split_axis=0, concat_axis=0, tiled=True)  88.9 us
    all_to_all x7, starting transfers between devices, exchange(): return lax.all_to_all(values, axis, split_axis=0, concat_axis=0, tiled=True)  40.2 us
    pallas_call x1, Pallas kernels, cache_partials(): pl.pallas_call(cache_kernel, out_shape=jax.ShapeDtypeStruct((groups, rows...  24.2 us
    psum x1, blocking collectives, body(): lax.psum(jnp.stack([jnp.sum(query_raw * query_raw, axis=1), jnp.sum(key_r...  14.9 us
    all_to_all x1, blocking collectives, exchange(): return lax.all_to_all(values, axis, split_axis=0, concat_axis=0, tiled=True)  13.7 us
    pallas_call x2, Pallas kernels, mix_columns(): pl.pallas_call(mix_kernel, out_shape=jax.ShapeDtypeStruct((parts, rows, c...  12.7 us
  transfers between devices with their start and end apart: 9, of which 8 were waited for; matrix products, arithmetic and copies ran while one was open for 5% of the time, Pallas kernels for 3%

profile of v3, /device:TPU:32, one launch (start us, length us, event | category | flops | bytes accessed | tf_op | source)
XLA Modules:
  0.0 369.0 jit_solution(10623558768594274510)
XLA Ops:
  7.2 4.8 %copy.64 = bf16[2048,3,256]{0,2,1:T(8,128)(2,1)} copy(bf16[2048,3,256]{2,0,1:T(8,128)(2,1)} %param.21) | data formatting | bytes 6291456 | tf_op args[2]
  12.2 2.9 fusion.23
  15.3 14.9 %psum.7 = f32[2,32]{1,0:T(2,128)S(1)} all-reduce(f32[2,32]{1,0:T(2,128)S(1)} %pad_maximum_fusion.6), channel_id=1, replica_groups=mesh['req'=32,'tp'=8] {'tp'}, use_global_device_ids=true, to_apply=%region_3.0 | all-reduce | flops 64 | bytes 512 | tf_op jit(solution)/shard_map/psum | solution.py:285
  32.8 11.2 %all-to-all-start = ((bf16[32,32,256]{2,1,0:T(8,128)(2,1)}), bf16[32,32,256]{2,1,0:T(8,128)(2,1)S(1)}, u32[]{:S(2)}, u32[]{:S(2)}) async-start(bf16[32,32,256]{2,1,0:T(8,128)(2,1)} %broadcast_in_dim.89), calls=%async_computation | async-start | bytes 1048576 | tf_op jit(solution)/shard_map/all_to_all | solution.py:188
  44.7 14.7 %all-to-all-done.q_ref = bf16[32,32,256]{2,1,0:T(8,128)(2,1)S(1)} async-done(((bf16[32,32,256]{2,1,0:T(8,128)(2,1)}), bf16[32,32,256]{2,1,0:T(8,128)(2,1)S(1)}, u32[]{:S(2)}, u32[]{:S(2)}) %all-to-all-start) | async-done | bytes 524320 | tf_op jit(solution)/shard_map/all_to_all | solution.py:188
  60.2 24.2 %shard_map.202 = bf16[32,32,384]{2,1,0:T(8,128)(2,1)} custom-call(s32[32]{0:T(128)} %groups_ref.1, s32[32]{0:T(128)} %index_ref.1, s32[32]{0:T(128)} %lengths_ref.1, bf16[32,32,256]{2,1,0:T(8,128)(2,1)} %copy-done.2, bf16[4096,256]{1,0:T(8,128)(2,1)} %k_ref.1, bf16[4096,256]{1,0:T(8,128)(2,1)} %v_ref.1), custom_call_target="tpu_custom_call" | custom-call | tf_op jit(solution)/shard_map/pallas_call | solution.py:126
  84.4 4.9 %all-to-all-start.1 = ((bf16[32,32,384]{2,1,0:T(8,128)(2,1)}), bf16[32,32,384]{2,1,0:T(8,128)(2,1)S(1)}, u32[]{:S(2)}, u32[]{:S(2)}) async-start(bf16[32,32,384]{2,1,0:T(8,128)(2,1)} %shard_map.202), calls=%async_computation.1 | async-start | bytes 1572864 | tf_op jit(solution)/shard_map/all_to_all | solution.py:188
  91.9 18.0 %all-to-all-done.1.part_ref = bf16[32,32,384]{2,1,0:T(8,128)(2,1)S(1)} async-done(((bf16[32,32,384]{2,1,0:T(8,128)(2,1)}), bf16[32,32,384]{2,1,0:T(8,128)(2,1)S(1)}, u32[]{:S(2)}, u32[]{:S(2)}) %all-to-all-start.1) | async-done | bytes 786464 | tf_op jit(solution)/shard_map/all_to_all | solution.py:188
  110.8 2.8 shard_map.203
  114.7 13.7 %all_to_all.40 = f32[8,4,2048]{2,1,0:T(4,128)S(1)} all-to-all(f32[8,4,2048]{2,1,0:T(4,128)S(1)} %reshape.441), channel_id=1, replica_groups=mesh['req'=32,'tp'=8] {'tp'}, dimensions={0} | all-to-all | bytes 524288 | tf_op jit(solution)/shard_map/all_to_all | solution.py:188
  129.1 3.4 all-to-all-start.3
  132.7 7.3 %all-to-all-done.3 = f32[8,4,2048]{2,1,0:T(4,128)S(1)} async-done(((f32[8,4,2048]{2,1,0:T(4,128)}), f32[8,4,2048]{2,1,0:T(4,128)S(1)}, u32[]{:S(2)}, u32[]{:S(2)}) %all-to-all-start.3) | async-done | bytes 262176 | tf_op jit(solution)/shard_map/all_to_all | solution.py:188
  143.9 5.1 %all-to-all-start.4 = ((f32[32,2,32]{2,1,0:T(2,128)}), f32[32,2,32]{2,1,0:T(2,128)S(1)}, u32[]{:S(2)}, u32[]{:S(2)}) async-start(f32[32,2,32]{2,1,0:T(2,128)} %bitcast.30), calls=%async_computation.4 | async-start | bytes 65536 | tf_op jit(solution)/shard_map/all_to_all | solution.py:188
  151.8 6.1 %all-to-all-done.4 = f32[32,2,32]{2,1,0:T(2,128)S(1)} async-done(((f32[32,2,32]{2,1,0:T(2,128)}), f32[32,2,32]{2,1,0:T(2,128)S(1)}, u32[]{:S(2)}, u32[]{:S(2)}) %all-to-all-start.4) | async-done | bytes 8224 | tf_op jit(solution)/shard_map/all_to_all | solution.py:188
  158.3 55.0 %all-gather.3.cloned.1.call-done = bf16[512,2048]{1,0:T(8,128)(2,1)} async-done(((bf16[16,2048]{1,0:T(8,128)(2,1)}), bf16[512,2048]{1,0:T(8,128)(2,1)}) %all-gather.3.cloned.1.call-update) | async-done | bytes 2097168 | tf_op jit(solution)/shard_map/all_gather | solution.py:337
  217.6 6.4 %shard_map.204 = bf16[8,512,256]{2,1,0:T(8,128)(2,1)} custom-call(bf16[512,256]{1,0:T(8,128)(2,1)} %pad_maximum_fusion.1.act_ref, bf16[256,2048]{1,0:T(8,128)(2,1)} %bitcast.131), custom_call_target="tpu_custom_call" | custom-call | tf_op jit(solution)/shard_map/pallas_call | solution.py:208
  223.9 4.3 %all-to-all-start.5 = ((bf16[8,512,256]{2,1,0:T(8,128)(2,1)}), bf16[8,512,256]{2,1,0:T(8,128)(2,1)S(1)}, u32[]{:S(2)}, u32[]{:S(2)}) async-start(bf16[8,512,256]{2,1,0:T(8,128)(2,1)} %shard_map.204), calls=%async_computation.5 | async-start | bytes 4194304 | tf_op jit(solution)/shard_map/all_to_all | solution.py:188
  228.4 62.7 %all-gather.5.cloned.1.call-done = bf16[512,2048]{1,0:T(8,128)(2,1)} async-done(((bf16[16,2048]{1,0:T(8,128)(2,1)}), bf16[512,2048]{1,0:T(8,128)(2,1)}) %all-gather.5.cloned.1.call-update) | async-done | bytes 2097168 | tf_op jit(solution)/shard_map/all_gather | solution.py:337
  291.1 2.7 fusion.6
  295.5 6.3 %shard_map.205 = bf16[8,512,256]{2,1,0:T(8,128)(2,1)} custom-call(bf16[512,256]{1,0:T(8,128)(2,1)} %pad_maximum_fusion.2.act_ref, bf16[256,2048]{1,0:T(8,128)(2,1)} %bitcast.132), custom_call_target="tpu_custom_call" | custom-call | tf_op jit(solution)/shard_map/pallas_call | solution.py:208
  301.9 4.4 %all-to-all-start.6 = ((bf16[8,512,256]{2,1,0:T(8,128)(2,1)}), bf16[8,512,256]{2,1,0:T(8,128)(2,1)}, u32[]{:S(2)}, u32[]{:S(2)}) async-start(bf16[8,512,256]{2,1,0:T(8,128)(2,1)} %shard_map.205), calls=%async_computation.6 | async-start | bytes 4194304 | tf_op jit(solution)/shard_map/all_to_all | solution.py:188
  306.6 26.8 %all-to-all-done.6 = bf16[8,512,256]{2,1,0:T(8,128)(2,1)} async-done(((bf16[8,512,256]{2,1,0:T(8,128)(2,1)}), bf16[8,512,256]{2,1,0:T(8,128)(2,1)}, u32[]{:S(2)}, u32[]{:S(2)}) %all-to-all-start.6) | async-done | bytes 2097184 | tf_op jit(solution)/shard_map/all_to_all | solution.py:188
  336.3 6.9 %all-to-all-start.7 = ((bf16[32,32,256]{2,1,0:T(8,128)(2,1)}), bf16[32,32,256]{2,1,0:T(8,128)(2,1)S(1)}, u32[]{:S(2)}, u32[]{:S(2)}) async-start(bf16[32,32,256]{2,1,0:T(8,128)(2,1)} %pad_maximum_fusion), calls=%async_computation.7 | async-start | bytes 1048576 | tf_op jit(solution)/shard_map/all_to_all | solution.py:188
  344.7 15.9 %all-to-all-done.7 = bf16[32,32,256]{2,1,0:T(8,128)(2,1)S(1)} async-done(((bf16[32,32,256]{2,1,0:T(8,128)(2,1)}), bf16[32,32,256]{2,1,0:T(8,128)(2,1)S(1)}, u32[]{:S(2)}, u32[]{:S(2)}) %all-to-all-start.7) | async-done | bytes 524320 | tf_op jit(solution)/shard_map/all_to_all | solution.py:188
  (144 shorter events, 28.4 us)
Async XLA Ops:
  7.2 106.4 %copy-start = (bf16[256,2048]{1,0:T(8,128)(2,1)S(1)}, bf16[256,2048]{1,0:T(8,128)(2,1)}, u32[]{:S(2)}) copy-start(bf16[256,2048]{1,0:T(8,128)(2,1)} %param.24) | copy-start | bytes 3145732
  12.0 18.1 %copy-start.17 = (f32[256]{0:T(256)S(1)}, f32[256]{0:T(256)}, u32[]{:S(2)}) copy-start(f32[256]{0:T(256)} %param.23) | copy-start | bytes 3076
  12.0 18.1 %copy-start.18 = (f32[256]{0:T(256)S(1)}, f32[256]{0:T(256)}, u32[]{:S(2)}) copy-start(f32[256]{0:T(256)} %param.22) | copy-start | bytes 3076
  12.0 18.3 %copy-start.19 = (s32[32]{0:T(128)S(1)}, s32[32]{0:T(128)}, u32[]{:S(2)}) copy-start(s32[32]{0:T(128)} %lengths_ref.1) | copy-start | bytes 388
  12.2 31.9 %copy-start.16 = (s32[4,8]{1,0:T(4,128)S(1)}, s32[4,8]{1,0:T(4,128)}, u32[]{:S(2)}) copy-start(s32[4,8]{1,0:T(4,128)} %param.33) | copy-start | bytes 388
  32.0 52.4 %copy-start.10 = (bf16[4,8,2,128]{3,1,2,0:T(8,128)(2,1)}, bf16[4,8,2,128]{3,1,2,0:T(8,128)(2,1)S(1)}, u32[]{:S(2)}) copy-start(bf16[4,8,2,128]{3,1,2,0:T(8,128)(2,1)S(1)} %copy.112) | copy-start | bytes 49156
  32.8 26.6 %all-to-all-start = ((bf16[32,32,256]{2,1,0:T(8,128)(2,1)}), bf16[32,32,256]{2,1,0:T(8,128)(2,1)S(1)}, u32[]{:S(2)}, u32[]{:S(2)}) async-start(bf16[32,32,256]{2,1,0:T(8,128)(2,1)} %broadcast_in_dim.89), calls=%async_computation | async-start | bytes 1048576 | tf_op jit(solution)/shard_map/all_to_all | solution.py:188
  44.7 45.5 %copy-start.12 = (bf16[8,4,256]{2,1,0:T(4,128)(2,1)S(1)}, bf16[8,4,256]{2,1,0:T(4,128)(2,1)}, u32[]{:S(2)}) copy-start(bf16[8,4,256]{2,1,0:T(4,128)(2,1)} %param.31) | copy-start | bytes 49156
  44.7 45.5 %copy-start.13 = (bf16[8,4,256]{2,1,0:T(4,128)(2,1)S(1)}, bf16[8,4,256]{2,1,0:T(4,128)(2,1)}, u32[]{:S(2)}) copy-start(bf16[8,4,256]{2,1,0:T(4,128)(2,1)} %param.32) | copy-start | bytes 49156
  84.4 25.5 %all-to-all-start.1 = ((bf16[32,32,384]{2,1,0:T(8,128)(2,1)}), bf16[32,32,384]{2,1,0:T(8,128)(2,1)S(1)}, u32[]{:S(2)}, u32[]{:S(2)}) async-start(bf16[32,32,384]{2,1,0:T(8,128)(2,1)} %shard_map.202), calls=%async_computation.1 | async-start | bytes 1572864 | tf_op jit(solution)/shard_map/all_to_all | solution.py:188
  91.9 18.0 %copy-start.8 = (bf16[64,256]{1,0:T(8,128)(2,1)}, bf16[64,256]{1,0:T(8,128)(2,1)S(1)}, u32[]{:S(2)}) copy-start(bf16[64,256]{1,0:T(8,128)(2,1)S(1)} %bitcast_dynamic-update-slice_fusion.k_ref) | copy-start | bytes 98308
  114.5 25.8 %copy-start.15 = (f32[2048]{0:T(1024)S(1)}, f32[2048]{0:T(1024)}, u32[]{:S(2)}) copy-start(f32[2048]{0:T(1024)} %param.25) | copy-start | bytes 24580
  114.6 27.9 %copy-start.11 = (s32[4,8,8]{2,1,0:T(8,128)S(1)}, s32[4,8,8]{2,1,0:T(8,128)}, u32[]{:S(2)}) copy-start(s32[4,8,8]{2,1,0:T(8,128)} %param.34) | copy-start | bytes 3076
  114.6 28.0 %copy-start.7 = (bf16[2048,64]{0,1:T(8,128)(2,1)S(1)}, bf16[2048,64]{0,1:T(8,128)(2,1)}, u32[]{:S(2)}) copy-start(bf16[2048,64]{0,1:T(8,128)(2,1)} %param.26) | copy-start | bytes 786436
  129.1 10.9 %all-to-all-start.3 = ((f32[8,4,2048]{2,1,0:T(4,128)}), f32[8,4,2048]{2,1,0:T(4,128)S(1)}, u32[]{:S(2)}, u32[]{:S(2)}) async-start(f32[8,4,2048]{2,1,0:T(4,128)} %broadcast_in_dim.98), calls=%async_computation.3 | async-start | bytes 524288 | tf_op jit(solution)/shard_map/all_to_all | solution.py:188
  132.5 80.8 %all-gather.3.cloned.1.call-start = ((), (), s32[]{:S(2)}) async-start(), calls=%async_computation.8 | async-start | bytes 2162688 | tf_op jit(solution)/shard_map/all_gather | solution.py:337
  141.7 149.3 %all-gather.5.cloned.1.call-start = ((), (), s32[]{:S(2)}) async-start(), calls=%async_computation.9 | async-start | bytes 2162688 | tf_op jit(solution)/shard_map/all_gather | solution.py:337
  143.9 13.9 %all-to-all-start.4 = ((f32[32,2,32]{2,1,0:T(2,128)}), f32[32,2,32]{2,1,0:T(2,128)S(1)}, u32[]{:S(2)}, u32[]{:S(2)}) async-start(f32[32,2,32]{2,1,0:T(2,128)} %bitcast.30), calls=%async_computation.4 | async-start | bytes 65536 | tf_op jit(solution)/shard_map/all_to_all | solution.py:188
  151.8 64.0 %copy-start.6 = (bf16[1,2048,2,128]{3,2,1,0:T(2,128)(2,1)}, bf16[1,2048,2,128]{3,2,1,0:T(2,128)(2,1)S(1)}, u32[]{:S(2)}) copy-start(bf16[1,2048,2,128]{3,2,1,0:T(2,128)(2,1)S(1)} %get-tuple-element.16) | copy-start | bytes 3145732
  151.8 64.2 %copy-start.4 = (bf16[1,2048,2,128]{3,2,1,0:T(2,128)(2,1)}, bf16[1,2048,2,128]{3,2,1,0:T(2,128)(2,1)S(1)}, u32[]{:S(2)}) copy-start(bf16[1,2048,2,128]{3,2,1,0:T(2,128)(2,1)S(1)} %get-tuple-element.17) | copy-start | bytes 3145732
  223.9 77.9 %all-to-all-start.5 = ((bf16[8,512,256]{2,1,0:T(8,128)(2,1)}), bf16[8,512,256]{2,1,0:T(8,128)(2,1)S(1)}, u32[]{:S(2)}, u32[]{:S(2)}) async-start(bf16[8,512,256]{2,1,0:T(8,128)(2,1)} %shard_map.204), calls=%async_computation.5 | async-start | bytes 4194304 | tf_op jit(solution)/shard_map/all_to_all | solution.py:188
  301.9 31.6 %all-to-all-start.6 = ((bf16[8,512,256]{2,1,0:T(8,128)(2,1)}), bf16[8,512,256]{2,1,0:T(8,128)(2,1)}, u32[]{:S(2)}, u32[]{:S(2)}) async-start(bf16[8,512,256]{2,1,0:T(8,128)(2,1)} %shard_map.205), calls=%async_computation.6 | async-start | bytes 4194304 | tf_op jit(solution)/shard_map/all_to_all | solution.py:188
  306.6 37.4 %copy-start.9 = (bf16[64,256]{1,0:T(8,128)(2,1)S(1)}, bf16[64,256]{1,0:T(8,128)(2,1)}, u32[]{:S(2)}) copy-start(bf16[64,256]{1,0:T(8,128)(2,1)} %copy-done.8) | copy-start | bytes 98308
  336.3 24.4 %all-to-all-start.7 = ((bf16[32,32,256]{2,1,0:T(8,128)(2,1)}), bf16[32,32,256]{2,1,0:T(8,128)(2,1)S(1)}, u32[]{:S(2)}, u32[]{:S(2)}) async-start(bf16[32,32,256]{2,1,0:T(8,128)(2,1)} %pad_maximum_fusion), calls=%async_computation.7 | async-start | bytes 1048576 | tf_op jit(solution)/shard_map/all_to_all | solution.py:188
  (7 other events, 19.8 us)
Sparse Core Ops, SparseCore 0:
  141.9 71.4 all-gather.2
  215.9 75.0 all-gather.4
